TPU v7x, 512 devices: a whole 4x4x16 slice. The times are simulated.
512 devices in a mesh: cell: 64 (over z, y_lo, core), coef: 8 (over y_hi, x).
Axes of the slice: x: 4, y: 4 (y_hi: 2, y_lo: 2; y = y_hi * 2 + y_lo), z: 16, core: 2. Of those that a mesh axis runs over, the one named last changes fastest.
Arguments:
- multipoles: bfloat16 [4096, 9, 1024], P('cell', None, 'coef'), may hold values from -6 to 6
- rotation: bfloat16 [4, 8, 128, 128], P(None, 'coef')
- coaxial: bfloat16 [40, 8, 128, 128], P(None, 'coef')
- offsets: int32 [40], replicated, may hold values from -128 to 128, as said below
- class_index: int32 [40], replicated, may hold values from 0 to 3, as said below
Outputs:
- local_field: bfloat16 [4096, 9, 1024], P('cell', None, 'coef')
Inputs may be any that keep to these rules, and one draw needn't show every extreme that they name: The offsets are distinct and nonzero, and both 128 and -128 occur. `class_index`: each class is named by exactly 10 offsets.
All inputs are finite; a program needn't handle non-finite values.
Results may differ from a plain program's by a relative error of at most 0.0057.
Values may be sent and summed in bfloat16 or wider, within the bound.
A program may use at most 64 MiB of HBM per device.

v0:
```python
import jax
import jax.numpy as jnp
import numpy as np
from jax import lax
from jax.sharding import PartitionSpec as P

NCLASS = 4


def passed_along(value, axis, steps):
    count = lax.axis_size(axis)
    pairs = [(source, (source + steps) % count) for source in range(count)]
    return lax.ppermute(value, axis, pairs)


def layout_tables():
    degree_list = []
    for block_number in range(8):
        for level_value in (block_number, 15 - block_number, 16 + block_number, 31 - block_number):
            for order_value in range(-level_value, level_value + 1):
                degree_list.append((level_value, order_value))
    order_list = []
    for block_number in range(8):
        if block_number == 0:
            magnitudes = (0, 16, 8, 24)
        else:
            magnitudes = (block_number, 32 - block_number, 16 - block_number, 16 + block_number)
        for size_m in magnitudes:
            signed_list = [size_m] if size_m == 0 else [size_m, -size_m]
            for order_value in signed_list:
                for level_value in range(size_m, 32):
                    order_list.append((level_value, order_value))
    position = {}
    for entry_index, entry_pair in enumerate(degree_list):
        position[entry_pair] = entry_index
    to_orders = np.array([position[entry_pair] for entry_pair in order_list], dtype=np.int32)
    to_degrees = np.argsort(to_orders).astype(np.int32)
    levels = np.array([entry_pair[0] for entry_pair in degree_list]).reshape(8, 128)
    orders = np.array([entry_pair[1] for entry_pair in order_list]).reshape(8, 128)
    same_level = (levels[:, :, None] == levels[:, None, :]).astype(np.float32)
    same_order = (orders[:, :, None] == orders[:, None, :]).astype(np.float32)
    return (to_orders, to_degrees, same_level, same_order)


def packing_tables(target_of, device_count):
    width = 1024 // device_count
    lists = [[[] for dest_number in range(device_count)] for src_number in range(device_count)]
    for target_pos in range(1024):
        source_pos = int(target_of[target_pos])
        lists[source_pos // width][target_pos // width].append((target_pos, source_pos))
    slot_count = max(
        (
            len(lists[src_number][dest_number])
            for src_number in range(device_count)
            for dest_number in range(device_count)
        )
    )
    send_table = np.zeros((device_count, device_count, slot_count), dtype=np.int32)
    recv_table = np.zeros((device_count, width), dtype=np.int32)
    for src_number in range(device_count):
        for dest_number in range(device_count):
            for slot_number, entry_pair in enumerate(lists[src_number][dest_number]):
                send_table[src_number, dest_number, slot_number] = (
                    entry_pair[1] - src_number * width
                )
                recv_table[dest_number, entry_pair[0] - dest_number * width] = (
                    src_number * slot_count + slot_number
                )
    return (send_table, recv_table, slot_count)


def on_device(multipoles, rotation, coaxial, offsets, class_index):
    to_orders, to_degrees, same_level, same_order = layout_tables()
    coef_count = lax.axis_size("coef")
    coef_rank = lax.axis_index("coef")
    blocks = 8 // coef_count
    first_block = coef_rank * blocks
    level_mask = lax.dynamic_slice_in_dim(
        jnp.asarray(same_level, jnp.bfloat16), first_block, blocks, 0
    )
    order_mask = lax.dynamic_slice_in_dim(
        jnp.asarray(same_order, jnp.bfloat16), first_block, blocks, 0
    )
    turning = rotation * level_mask[None]
    moving = coaxial * order_mask[None]
    cell_count = multipoles.shape[0]
    columns = multipoles.shape[2]
    per_class = class_index.shape[0] // NCLASS
    grouped = jnp.argsort(class_index, stable=True).reshape(NCLASS, per_class)
    send_fwd, recv_fwd, slots_fwd = packing_tables(to_orders, coef_count)
    send_bwd, recv_bwd, slots_bwd = packing_tables(to_degrees, coef_count)
    own_send_fwd = lax.dynamic_index_in_dim(
        jnp.asarray(send_fwd), coef_rank, 0, keepdims=False
    ).reshape(-1)
    own_recv_fwd = lax.dynamic_index_in_dim(jnp.asarray(recv_fwd), coef_rank, 0, keepdims=False)
    own_send_bwd = lax.dynamic_index_in_dim(
        jnp.asarray(send_bwd), coef_rank, 0, keepdims=False
    ).reshape(-1)
    own_recv_bwd = lax.dynamic_index_in_dim(jnp.asarray(recv_bwd), coef_rank, 0, keepdims=False)
    degree_rows = multipoles[None]
    batches = [[class_number] for class_number in range(NCLASS)]
    field_sum = jnp.zeros((cell_count, 9, blocks, 128), jnp.float32)
    for members in batches:
        class_rows = jnp.asarray(np.array(members, dtype=np.int32))
        matrices = turning[np.array(members, dtype=np.int32)]
        turn_shaped = degree_rows.reshape(
            degree_rows.shape[0], degree_rows.shape[1], 9, blocks, 128
        )
        if degree_rows.shape[0] == matrices.shape[0]:
            result = jnp.einsum(
                "bnsgj,bgij->bnsgi", turn_shaped, matrices, preferred_element_type=jnp.float32
            )
        else:
            result = jnp.einsum(
                "nsgj,bgij->bnsgi", turn_shaped[0], matrices, preferred_element_type=jnp.float32
            )
        to_degree_rows = result.reshape(matrices.shape[0], degree_rows.shape[1], 9, columns).astype(
            jnp.bfloat16
        )
        to_lead = to_degree_rows.shape[0:3]
        to_packed = jnp.take(to_degree_rows, own_send_fwd, axis=3).reshape(
            to_lead + (coef_count, slots_fwd)
        )
        to_moved = lax.all_to_all(to_packed, "coef", split_axis=3, concat_axis=3, tiled=True)
        near_rows = jnp.take(
            to_moved.reshape(to_lead + (coef_count * slots_fwd,)), own_recv_fwd, axis=3
        )
        beside = {}
        for direction in (1, -1):
            for distance in (1, 2):
                beside[-direction * distance] = passed_along(
                    near_rows, "cell", direction * distance
                )
        extended = jnp.concatenate(
            [beside[-2], beside[-1], near_rows, beside[1], beside[2]], axis=1
        )
        batch_size = class_rows.shape[0]

        def add_offset(position_index, carried):
            chosen = grouped[class_rows, position_index]
            starts = 2 * cell_count + offsets[chosen]
            shifted = jax.vmap(
                lambda source_rows, start_cell: lax.dynamic_slice_in_dim(
                    source_rows, start_cell, cell_count, 0
                )
            )(extended, starts)
            shaped = shifted.reshape(batch_size, cell_count, 9, blocks, 128)
            return carried + jnp.einsum(
                "bnsgj,bgij->bnsgi", shaped, moving[chosen], preferred_element_type=jnp.float32
            )

        start_sum = jnp.zeros((batch_size, cell_count, 9, blocks, 128), jnp.float32)
        summed = lax.fori_loop(0, per_class, add_offset, start_sum)
        order_rows = summed.reshape(batch_size, cell_count, 9, columns).astype(jnp.bfloat16)
        lead = order_rows.shape[0:3]
        packed = jnp.take(order_rows, own_send_bwd, axis=3).reshape(lead + (coef_count, slots_bwd))
        moved = lax.all_to_all(packed, "coef", split_axis=3, concat_axis=3, tiled=True)
        returned = jnp.take(moved.reshape(lead + (coef_count * slots_bwd,)), own_recv_bwd, axis=3)
        shaped = returned.reshape(len(members), cell_count, 9, blocks, 128)
        field_sum = field_sum + jnp.einsum(
            "bnsgi,bgij->nsgj", shaped, matrices, preferred_element_type=jnp.float32
        )
    return field_sum.reshape(cell_count, 9, columns).astype(jnp.bfloat16)


def solution(mesh):
    placed = (
        P("cell", None, "coef"),
        P(None, "coef", None, None),
        P(None, "coef", None, None),
        P(),
        P(),
    )
    return jax.shard_map(
        on_device, mesh=mesh, in_specs=placed, out_specs=P("cell", None, "coef"), check_vma=False
    )
```

profile of v0, /device:TPU:2, one launch (start us, length us, event | category | flops | bytes accessed | tf_op | source)
XLA Modules:
  0.0 496.5 jit_solution(4002700607880476264)
XLA Ops:
  12.4 9.2 %all-to-all-start = ((bf16[8,2,4608]{2,1,0:T(2,128)(2,1)}), bf16[8,2,4608]{2,1,0:T(2,128)(2,1)S(1)}, u32[]{:S(2)}, u32[]{:S(2)}) async-start(bf16[8,2,4608]{2,1,0:T(2,128)(2,1)} %reshape.1163), calls=%async_computation | async-start | bytes 294912 | tf_op jit(solution)/shard_map/all_to_all | solution.py:124
  22.5 6.1 %all-to-all-done = bf16[8,2,4608]{2,1,0:T(2,128)(2,1)S(1)} async-done(((bf16[8,2,4608]{2,1,0:T(2,128)(2,1)}), bf16[8,2,4608]{2,1,0:T(2,128)(2,1)S(1)}, u32[]{:S(2)}, u32[]{:S(2)}) %all-to-all-start) | async-done | bytes 147488 | tf_op jit(solution)/shard_map/all_to_all | solution.py:124
  28.6 4.4 all-to-all-start.2
  34.0 6.1 %all-to-all-done.2 = bf16[8,2,4608]{2,1,0:T(2,128)(2,1)S(1)} async-done(((bf16[8,2,4608]{2,1,0:T(2,128)(2,1)}), bf16[8,2,4608]{2,1,0:T(2,128)(2,1)S(1)}, u32[]{:S(2)}, u32[]{:S(2)}) %all-to-all-start.2) | async-done | bytes 147488 | tf_op jit(solution)/shard_map/all_to_all | solution.py:124
  40.1 4.4 all-to-all-start.4
  46.3 5.3 %all-to-all-done.4 = bf16[8,2,4608]{2,1,0:T(2,128)(2,1)S(1)} async-done(((bf16[8,2,4608]{2,1,0:T(2,128)(2,1)}), bf16[8,2,4608]{2,1,0:T(2,128)(2,1)S(1)}, u32[]{:S(2)}, u32[]{:S(2)}) %all-to-all-start.4) | async-done | bytes 147488 | tf_op jit(solution)/shard_map/all_to_all | solution.py:124
  52.3 5.0 %all-to-all-start.6 = ((bf16[8,2,4608]{2,1,0:T(2,128)(2,1)}), bf16[8,2,4608]{2,1,0:T(2,128)(2,1)}, u32[]{:S(2)}, u32[]{:S(2)}) async-start(bf16[8,2,4608]{2,1,0:T(2,128)(2,1)} %reshape.1175), calls=%async_computation.6 | async-start | bytes 294912 | tf_op jit(solution)/shard_map/all_to_all | solution.py:124
  67.4 2.6 bitcast_select_fusion.2
  74.6 2.0 sort.17
  78.7 5.7 %collective-permute-start.2 = (bf16[1,64,9,128]{1,2,3,0:T(8,128)(2,1)}, bf16[1,64,9,128]{1,2,3,0:T(8,128)(2,1)}, u32[]{:S(2)}, u32[]{:S(2)}) collective-permute-start(bf16[1,64,9,128]{1,2,3,0:T(8,128)(2,1)} %get-tuple-element.1303), channel_id=1, source_target_pairs={{0,504},{8,0},{16,8},{24,16},{32,24},{40,32},{48,40},{56,48},{64,5... | collective-permute-start | bytes 442376 | tf_op jit(solution)/shard_map/ppermute | solution.py:13
  84.5 7.6 %collective-permute-start.3 = (bf16[1,64,9,128]{1,2,3,0:T(8,128)(2,1)}, bf16[1,64,9,128]{1,2,3,0:T(8,128)(2,1)}, u32[]{:S(2)}, u32[]{:S(2)}) collective-permute-start(bf16[1,64,9,128]{1,2,3,0:T(8,128)(2,1)} %get-tuple-element.1303), channel_id=1, source_target_pairs={{0,496},{8,504},{16,0},{24,8},{32,16},{40,24},{48,32},{56,40},{64,... | collective-permute-start | bytes 442376 | tf_op jit(solution)/shard_map/ppermute | solution.py:13
  94.0 2.0 copy.95
  103.9 5.7 %collective-permute-start.10 = (bf16[1,64,9,128]{1,2,3,0:T(8,128)(2,1)}, bf16[1,64,9,128]{1,2,3,0:T(8,128)(2,1)}, u32[]{:S(2)}, u32[]{:S(2)}) collective-permute-start(bf16[1,64,9,128]{1,2,3,0:T(8,128)(2,1)} %get-tuple-element.1302), channel_id=1, source_target_pairs={{0,504},{8,0},{16,8},{24,16},{32,24},{40,32},{48,40},{56,48},{64,5... | collective-permute-start | bytes 442376 | tf_op jit(solution)/shard_map/ppermute | solution.py:13
  114.8 11.0 %collective-permute-start.11 = (bf16[1,64,9,128]{1,2,3,0:T(8,128)(2,1)}, bf16[1,64,9,128]{1,2,3,0:T(8,128)(2,1)}, u32[]{:S(2)}, u32[]{:S(2)}) collective-permute-start(bf16[1,64,9,128]{1,2,3,0:T(8,128)(2,1)} %get-tuple-element.1302), channel_id=1, source_target_pairs={{0,496},{8,504},{16,0},{24,8},{32,16},{40,24},{48,32},{56,40},{64,... | collective-permute-start | bytes 442376 | tf_op jit(solution)/shard_map/ppermute | solution.py:13
  135.0 55.8 %while.120 = (s32[]{:T(128)}, f32[1,64,9,1,128]{4,1,2,3,0:T(8,128)S(1)}, s32[4,10]{1,0:T(4,128)S(1)}, bf16[40,1,128,128]{3,2,1,0:T(8,128)(2,1)S(1)}, s32[40]{0:T...) while((s32[]{:T(128)}, ...), condition=%wide.region_2.4_spmd.clone.clone, body=%wide.region_1.3_spmd.sunk.clone.clone.sunk | while | flops 19021832 | bytes 771303 | solution.py:153
  196.3 5.7 %collective-permute-start.6 = (bf16[1,64,9,128]{1,2,3,0:T(8,128)(2,1)}, bf16[1,64,9,128]{1,2,3,0:T(8,128)(2,1)}, u32[]{:S(2)}, u32[]{:S(2)}) collective-permute-start(bf16[1,64,9,128]{1,2,3,0:T(8,128)(2,1)} %get-tuple-element.1301), channel_id=1, source_target_pairs={{0,504},{8,0},{16,8},{24,16},{32,24},{40,32},{48,40},{56,48},{64,5... | collective-permute-start | bytes 442376 | tf_op jit(solution)/shard_map/ppermute | solution.py:13
  207.3 4.1 collective-permute-start.7
  220.5 56.4 %while.122 = (s32[]{:T(128)}, f32[1,64,9,1,128]{4,1,2,3,0:T(8,128)S(1)}, s32[4,10]{1,0:T(4,128)S(1)}, bf16[40,1,128,128]{3,2,1,0:T(8,128)(2,1)S(1)}, s32[40]{0:T...) while((s32[]{:T(128)}, ...), condition=%wide.region_6.8_spmd.clone.clone, body=%wide.region_5.7_spmd.sunk.clone.clone.sunk | while | flops 19021832 | bytes 771303 | solution.py:153
  282.5 5.7 %collective-permute-start.14 = (bf16[1,64,9,128]{1,2,3,0:T(8,128)(2,1)S(1)}, bf16[1,64,9,128]{1,2,3,0:T(8,128)(2,1)}, u32[]{:S(2)}, u32[]{:S(2)}) collective-permute-start(bf16[1,64,9,128]{1,2,3,0:T(8,128)(2,1)S(1)} %get-tuple-element.1300), channel_id=1, source_target_pairs={{0,504},{8,0},{16,8},{24,16},{32,24},{40,32},{48,40},{56,48},{64,5... | collective-permute-start | bytes 442376 | tf_op jit(solution)/shard_map/ppermute | solution.py:13
  293.4 3.9 collective-permute-start.15
  304.5 56.5 %while.121 = (s32[]{:T(128)}, f32[1,64,9,1,128]{4,1,2,3,0:T(8,128)S(1)}, s32[4,10]{1,0:T(4,128)S(1)}, bf16[40,1,128,128]{3,2,1,0:T(8,128)(2,1)S(1)}, s32[40]{0:T...) while((s32[]{:T(128)}, ...), condition=%wide.region_4.6_spmd.clone.clone, body=%wide.region_3.5_spmd.sunk.clone.clone.sunk | while | flops 19021832 | bytes 771303 | solution.py:153
  373.2 2.5 gather_fusion.10
  376.9 2.5 gather_fusion.6
  383.5 56.3 %while.123 = (s32[]{:T(128)}, f32[1,64,9,1,128]{4,1,2,3,0:T(8,128)S(1)}, s32[4,10]{1,0:T(4,128)S(1)}, bf16[40,1,128,128]{3,2,1,0:T(8,128)(2,1)S(1)}, s32[40]{0:T...) while((s32[]{:T(128)}, ...), condition=%wide.region_8.10_spmd.clone.clone, body=%wide.region_7.9_spmd.sunk.clone.clone.sunk | while | flops 19021832 | bytes 771303 | solution.py:153
  444.2 7.6 %all-to-all-start.1 = ((bf16[8,2,4608]{2,1,0:T(2,128)(2,1)}), bf16[8,2,4608]{2,1,0:T(2,128)(2,1)S(1)}, u32[]{:S(2)}, u32[]{:S(2)}) async-start(bf16[8,2,4608]{2,1,0:T(2,128)(2,1)} %reshape.1165), calls=%async_computation.1 | async-start | bytes 294912 | tf_op jit(solution)/shard_map/all_to_all | solution.py:157
  452.7 6.0 %all-to-all-done.1 = bf16[8,2,4608]{2,1,0:T(2,128)(2,1)S(1)} async-done(((bf16[8,2,4608]{2,1,0:T(2,128)(2,1)}), bf16[8,2,4608]{2,1,0:T(2,128)(2,1)S(1)}, u32[]{:S(2)}, u32[]{:S(2)}) %all-to-all-start.1) | async-done | bytes 147488 | tf_op jit(solution)/shard_map/all_to_all | solution.py:157
  458.8 4.4 all-to-all-start.3
  464.2 6.1 %all-to-all-done.3 = bf16[8,2,4608]{2,1,0:T(2,128)(2,1)S(1)} async-done(((bf16[8,2,4608]{2,1,0:T(2,128)(2,1)}), bf16[8,2,4608]{2,1,0:T(2,128)(2,1)S(1)}, u32[]{:S(2)}, u32[]{:S(2)}) %all-to-all-start.3) | async-done | bytes 147488 | tf_op jit(solution)/shard_map/all_to_all | solution.py:157
  470.3 4.4 all-to-all-start.5
  475.7 6.1 %all-to-all-done.5 = bf16[8,2,4608]{2,1,0:T(2,128)(2,1)S(1)} async-done(((bf16[8,2,4608]{2,1,0:T(2,128)(2,1)}), bf16[8,2,4608]{2,1,0:T(2,128)(2,1)S(1)}, u32[]{:S(2)}, u32[]{:S(2)}) %all-to-all-start.5) | async-done | bytes 147488 | tf_op jit(solution)/shard_map/all_to_all | solution.py:157
  481.8 4.4 all-to-all-start.7
  489.8 3.5 all-to-all-done.7
  (294 shorter events, 221.8 us)
Async XLA Ops:
  0.0 1.7 copy-start
  12.4 16.2 %all-to-all-start = ((bf16[8,2,4608]{2,1,0:T(2,128)(2,1)}), bf16[8,2,4608]{2,1,0:T(2,128)(2,1)S(1)}, u32[]{:S(2)}, u32[]{:S(2)}) async-start(bf16[8,2,4608]{2,1,0:T(2,128)(2,1)} %reshape.1163), calls=%async_computation | async-start | bytes 294912 | tf_op jit(solution)/shard_map/all_to_all | solution.py:124
  28.6 11.5 %all-to-all-start.2 = ((bf16[8,2,4608]{2,1,0:T(2,128)(2,1)}), bf16[8,2,4608]{2,1,0:T(2,128)(2,1)S(1)}, u32[]{:S(2)}, u32[]{:S(2)}) async-start(bf16[8,2,4608]{2,1,0:T(2,128)(2,1)} %reshape.1167), calls=%async_computation.2 | async-start | bytes 294912 | tf_op jit(solution)/shard_map/all_to_all | solution.py:124
  33.2 24.2 %copy-start.1 = (bf16[40,1,128,128]{3,2,1,0:T(8,128)(2,1)S(1)}, bf16[40,1,128,128]{3,2,1,0:T(8,128)(2,1)}, u32[]{:S(2)}) copy-start(bf16[40,1,128,128]{3,2,1,0:T(8,128)(2,1)} %param.35) | copy-start | bytes 3932164
  40.1 11.5 %copy-start.3 = (bf16[8,2,4608]{2,1,0:T(2,128)(2,1)}, bf16[8,2,4608]{2,1,0:T(2,128)(2,1)S(1)}, u32[]{:S(2)}) copy-start(bf16[8,2,4608]{2,1,0:T(2,128)(2,1)S(1)} %all-to-all-done.2) | copy-start | bytes 442372
  40.1 11.5 %all-to-all-start.4 = ((bf16[8,2,4608]{2,1,0:T(2,128)(2,1)}), bf16[8,2,4608]{2,1,0:T(2,128)(2,1)S(1)}, u32[]{:S(2)}, u32[]{:S(2)}) async-start(bf16[8,2,4608]{2,1,0:T(2,128)(2,1)} %reshape.1171), calls=%async_computation.4 | async-start | bytes 294912 | tf_op jit(solution)/shard_map/all_to_all | solution.py:124
  51.6 0.7 copy-start.5
  52.3 12.2 %all-to-all-start.6 = ((bf16[8,2,4608]{2,1,0:T(2,128)(2,1)}), bf16[8,2,4608]{2,1,0:T(2,128)(2,1)}, u32[]{:S(2)}, u32[]{:S(2)}) async-start(bf16[8,2,4608]{2,1,0:T(2,128)(2,1)} %reshape.1175), calls=%async_computation.6 | async-start | bytes 294912 | tf_op jit(solution)/shard_map/all_to_all | solution.py:124
  57.4 0.9 copy-start.4
  67.4 7.2 %copy-start.6 = (s32[40]{0:T(128)S(1)}, s32[40]{0:T(128)}, u32[]{:S(2)}) copy-start(s32[40]{0:T(128)} %param.37) | copy-start | bytes 484
  70.0 28.3 %collective-permute-start = (bf16[1,64,9,128]{1,2,3,0:T(8,128)(2,1)}, bf16[1,64,9,128]{1,2,3,0:T(8,128)(2,1)}, u32[]{:S(2)}, u32[]{:S(2)}) collective-permute-start(bf16[1,64,9,128]{1,2,3,0:T(8,128)(2,1)} %get-tuple-element.1303), channel_id=1, source_target_pairs={{0,16},{8,24},{16,32},{24,40},{32,48},{40,56},{48,64},{56,72},{64,... | collective-permute-start | bytes 442376 | tf_op jit(solution)/shard_map/ppermute | solution.py:13
  72.6 31.2 %collective-permute-start.1 = (bf16[1,64,9,128]{1,2,3,0:T(8,128)(2,1)}, bf16[1,64,9,128]{1,2,3,0:T(8,128)(2,1)}, u32[]{:S(2)}, u32[]{:S(2)}) collective-permute-start(bf16[1,64,9,128]{1,2,3,0:T(8,128)(2,1)} %get-tuple-element.1303), channel_id=1, source_target_pairs={{0,8},{8,16},{16,24},{24,32},{32,40},{40,48},{48,56},{56,64},{64,7... | collective-permute-start | bytes 442376 | tf_op jit(solution)/shard_map/ppermute | solution.py:13
  78.7 36.1 %collective-permute-start.2 = (bf16[1,64,9,128]{1,2,3,0:T(8,128)(2,1)}, bf16[1,64,9,128]{1,2,3,0:T(8,128)(2,1)}, u32[]{:S(2)}, u32[]{:S(2)}) collective-permute-start(bf16[1,64,9,128]{1,2,3,0:T(8,128)(2,1)} %get-tuple-element.1303), channel_id=1, source_target_pairs={{0,504},{8,0},{16,8},{24,16},{32,24},{40,32},{48,40},{56,48},{64,5... | collective-permute-start | bytes 442376 | tf_op jit(solution)/shard_map/ppermute | solution.py:13
  84.5 45.0 %collective-permute-start.3 = (bf16[1,64,9,128]{1,2,3,0:T(8,128)(2,1)}, bf16[1,64,9,128]{1,2,3,0:T(8,128)(2,1)}, u32[]{:S(2)}, u32[]{:S(2)}) collective-permute-start(bf16[1,64,9,128]{1,2,3,0:T(8,128)(2,1)} %get-tuple-element.1303), channel_id=1, source_target_pairs={{0,496},{8,504},{16,0},{24,8},{32,16},{40,24},{48,32},{56,40},{64,... | collective-permute-start | bytes 442376 | tf_op jit(solution)/shard_map/ppermute | solution.py:13
  92.1 98.7 %collective-permute-start.8 = (bf16[1,64,9,128]{1,2,3,0:T(8,128)(2,1)}, bf16[1,64,9,128]{1,2,3,0:T(8,128)(2,1)}, u32[]{:S(2)}, u32[]{:S(2)}) collective-permute-start(bf16[1,64,9,128]{1,2,3,0:T(8,128)(2,1)} %get-tuple-element.1302), channel_id=1, source_target_pairs={{0,16},{8,24},{16,32},{24,40},{32,48},{40,56},{48,64},{56,72},{64,... | collective-permute-start | bytes 442376 | tf_op jit(solution)/shard_map/ppermute | solution.py:13
  98.3 98.0 %collective-permute-start.9 = (bf16[1,64,9,128]{1,2,3,0:T(8,128)(2,1)}, bf16[1,64,9,128]{1,2,3,0:T(8,128)(2,1)}, u32[]{:S(2)}, u32[]{:S(2)}) collective-permute-start(bf16[1,64,9,128]{1,2,3,0:T(8,128)(2,1)} %get-tuple-element.1302), channel_id=1, source_target_pairs={{0,8},{8,16},{16,24},{24,32},{32,40},{40,48},{48,56},{56,64},{64,7... | collective-permute-start | bytes 442376 | tf_op jit(solution)/shard_map/ppermute | solution.py:13
  103.9 103.4 %collective-permute-start.10 = (bf16[1,64,9,128]{1,2,3,0:T(8,128)(2,1)}, bf16[1,64,9,128]{1,2,3,0:T(8,128)(2,1)}, u32[]{:S(2)}, u32[]{:S(2)}) collective-permute-start(bf16[1,64,9,128]{1,2,3,0:T(8,128)(2,1)} %get-tuple-element.1302), channel_id=1, source_target_pairs={{0,504},{8,0},{16,8},{24,16},{32,24},{40,32},{48,40},{56,48},{64,5... | collective-permute-start | bytes 442376 | tf_op jit(solution)/shard_map/ppermute | solution.py:13
  111.6 23.4 %copy-start.7 = (s32[40]{0:T(128)S(1)}, s32[40]{0:T(128)}, u32[]{:S(2)}) copy-start(s32[40]{0:T(128)} %param.36) | copy-start | bytes 484
  114.8 100.1 %collective-permute-start.11 = (bf16[1,64,9,128]{1,2,3,0:T(8,128)(2,1)}, bf16[1,64,9,128]{1,2,3,0:T(8,128)(2,1)}, u32[]{:S(2)}, u32[]{:S(2)}) collective-permute-start(bf16[1,64,9,128]{1,2,3,0:T(8,128)(2,1)} %get-tuple-element.1302), channel_id=1, source_target_pairs={{0,496},{8,504},{16,0},{24,8},{32,16},{40,24},{48,32},{56,40},{64,... | collective-permute-start | bytes 442376 | tf_op jit(solution)/shard_map/ppermute | solution.py:13
  129.4 147.5 %collective-permute-start.4 = (bf16[1,64,9,128]{1,2,3,0:T(8,128)(2,1)}, bf16[1,64,9,128]{1,2,3,0:T(8,128)(2,1)}, u32[]{:S(2)}, u32[]{:S(2)}) collective-permute-start(bf16[1,64,9,128]{1,2,3,0:T(8,128)(2,1)} %get-tuple-element.1301), channel_id=1, source_target_pairs={{0,16},{8,24},{16,32},{24,40},{32,48},{40,56},{48,64},{56,72},{64,... | collective-permute-start | bytes 442376 | tf_op jit(solution)/shard_map/ppermute | solution.py:13
  190.8 91.7 %collective-permute-start.5 = (bf16[1,64,9,128]{1,2,3,0:T(8,128)(2,1)}, bf16[1,64,9,128]{1,2,3,0:T(8,128)(2,1)}, u32[]{:S(2)}, u32[]{:S(2)}) collective-permute-start(bf16[1,64,9,128]{1,2,3,0:T(8,128)(2,1)} %get-tuple-element.1301), channel_id=1, source_target_pairs={{0,8},{8,16},{16,24},{24,32},{32,40},{40,48},{48,56},{56,64},{64,7... | collective-permute-start | bytes 442376 | tf_op jit(solution)/shard_map/ppermute | solution.py:13
  196.3 97.1 %collective-permute-start.6 = (bf16[1,64,9,128]{1,2,3,0:T(8,128)(2,1)}, bf16[1,64,9,128]{1,2,3,0:T(8,128)(2,1)}, u32[]{:S(2)}, u32[]{:S(2)}) collective-permute-start(bf16[1,64,9,128]{1,2,3,0:T(8,128)(2,1)} %get-tuple-element.1301), channel_id=1, source_target_pairs={{0,504},{8,0},{16,8},{24,16},{32,24},{40,32},{48,40},{56,48},{64,5... | collective-permute-start | bytes 442376 | tf_op jit(solution)/shard_map/ppermute | solution.py:13
  207.3 93.7 %collective-permute-start.7 = (bf16[1,64,9,128]{1,2,3,0:T(8,128)(2,1)}, bf16[1,64,9,128]{1,2,3,0:T(8,128)(2,1)}, u32[]{:S(2)}, u32[]{:S(2)}) collective-permute-start(bf16[1,64,9,128]{1,2,3,0:T(8,128)(2,1)} %get-tuple-element.1301), channel_id=1, source_target_pairs={{0,496},{8,504},{16,0},{24,8},{32,16},{40,24},{48,32},{56,40},{64,... | collective-permute-start | bytes 442376 | tf_op jit(solution)/shard_map/ppermute | solution.py:13
  215.0 146.1 %collective-permute-start.12 = (bf16[1,64,9,128]{1,2,3,0:T(8,128)(2,1)S(1)}, bf16[1,64,9,128]{1,2,3,0:T(8,128)(2,1)}, u32[]{:S(2)}, u32[]{:S(2)}) collective-permute-start(bf16[1,64,9,128]{1,2,3,0:T(8,128)(2,1)S(1)} %get-tuple-element.1300), channel_id=1, source_target_pairs={{0,16},{8,24},{16,32},{24,40},{32,48},{40,56},{48,64},{56,72},{64,... | collective-permute-start | bytes 442376 | tf_op jit(solution)/shard_map/ppermute | solution.py:13
  276.9 87.7 %collective-permute-start.13 = (bf16[1,64,9,128]{1,2,3,0:T(8,128)(2,1)S(1)}, bf16[1,64,9,128]{1,2,3,0:T(8,128)(2,1)}, u32[]{:S(2)}, u32[]{:S(2)}) collective-permute-start(bf16[1,64,9,128]{1,2,3,0:T(8,128)(2,1)S(1)} %get-tuple-element.1300), channel_id=1, source_target_pairs={{0,8},{8,16},{16,24},{24,32},{32,40},{40,48},{48,56},{56,64},{64,7... | collective-permute-start | bytes 442376 | tf_op jit(solution)/shard_map/ppermute | solution.py:13
  282.5 97.0 %collective-permute-start.14 = (bf16[1,64,9,128]{1,2,3,0:T(8,128)(2,1)S(1)}, bf16[1,64,9,128]{1,2,3,0:T(8,128)(2,1)}, u32[]{:S(2)}, u32[]{:S(2)}) collective-permute-start(bf16[1,64,9,128]{1,2,3,0:T(8,128)(2,1)S(1)} %get-tuple-element.1300), channel_id=1, source_target_pairs={{0,504},{8,0},{16,8},{24,16},{32,24},{40,32},{48,40},{56,48},{64,5... | collective-permute-start | bytes 442376 | tf_op jit(solution)/shard_map/ppermute | solution.py:13
  293.4 88.1 %collective-permute-start.15 = (bf16[1,64,9,128]{1,2,3,0:T(8,128)(2,1)S(1)}, bf16[1,64,9,128]{1,2,3,0:T(8,128)(2,1)}, u32[]{:S(2)}, u32[]{:S(2)}) collective-permute-start(bf16[1,64,9,128]{1,2,3,0:T(8,128)(2,1)S(1)} %get-tuple-element.1300), channel_id=1, source_target_pairs={{0,496},{8,504},{16,0},{24,8},{32,16},{40,24},{48,32},{56,40},{64,... | collective-permute-start | bytes 442376 | tf_op jit(solution)/shard_map/ppermute | solution.py:13
  439.8 2.0 copy-start.2
  444.2 14.6 %all-to-all-start.1 = ((bf16[8,2,4608]{2,1,0:T(2,128)(2,1)}), bf16[8,2,4608]{2,1,0:T(2,128)(2,1)S(1)}, u32[]{:S(2)}, u32[]{:S(2)}) async-start(bf16[8,2,4608]{2,1,0:T(2,128)(2,1)} %reshape.1165), calls=%async_computation.1 | async-start | bytes 294912 | tf_op jit(solution)/shard_map/all_to_all | solution.py:157
  458.8 11.5 %all-to-all-start.3 = ((bf16[8,2,4608]{2,1,0:T(2,128)(2,1)}), bf16[8,2,4608]{2,1,0:T(2,128)(2,1)S(1)}, u32[]{:S(2)}, u32[]{:S(2)}) async-start(bf16[8,2,4608]{2,1,0:T(2,128)(2,1)} %reshape.1169), calls=%async_computation.3 | async-start | bytes 294912 | tf_op jit(solution)/shard_map/all_to_all | solution.py:157
  470.3 11.5 %all-to-all-start.5 = ((bf16[8,2,4608]{2,1,0:T(2,128)(2,1)}), bf16[8,2,4608]{2,1,0:T(2,128)(2,1)S(1)}, u32[]{:S(2)}, u32[]{:S(2)}) async-start(bf16[8,2,4608]{2,1,0:T(2,128)(2,1)} %reshape.1173), calls=%async_computation.5 | async-start | bytes 294912 | tf_op jit(solution)/shard_map/all_to_all | solution.py:157
  481.8 11.5 %all-to-all-start.7 = ((bf16[8,2,4608]{2,1,0:T(2,128)(2,1)}), bf16[8,2,4608]{2,1,0:T(2,128)(2,1)S(1)}, u32[]{:S(2)}, u32[]{:S(2)}) async-start(bf16[8,2,4608]{2,1,0:T(2,128)(2,1)} %reshape.1177), calls=%async_computation.7 | async-start | bytes 294912 | tf_op jit(solution)/shard_map/all_to_all | solution.py:157
where the time goes:
time: 502 us; the launch traced here: 497 us
  local copies, waits for them, and re-layouts  158 us (31%)
  loops' own time  129 us (26%)
  starting transfers between devices  109 us (22%)
  matrix products  49.2 us (10%)
  waiting for transfers between devices  40.5 us (8%)
  other arithmetic  10.1 us (2%)
    another operation x4, loops' own time, on_device(): summed = lax.fori_loop(0, per_class, add_offset, start_sum)  129 us
    ppermute x16, starting transfers between devices, passed_along(): return lax.ppermute(value, axis, pairs)  64.9 us
    dot_general x40, matrix products, add_offset(): jnp.einsum('bnsgj,bgij->bnsgi', shaped, moving[chosen], preferred_element...  46.7 us
    unnamed x48, local copies, waits for them, and re-layouts  35.6 us
    ppermute x16, local copies, waits for them, and re-layouts, passed_along(): return lax.ppermute(value, axis, pairs)  30.4 us
    gather x40, local copies, waits for them, and re-layouts, add_offset(): starts = 2 * cell_count + offsets[chosen]  25.5 us
    while x40, local copies, waits for them, and re-layouts, add_offset(): chosen = grouped[class_rows, position_index]  23.4 us
    all_to_all x4, starting transfers between devices, on_device(): lax.all_to_all(to_packed, 'coef', split_axis=3, concat_axis=3, tiled=True)  23.1 us
  transfers between devices with their start and end apart: 24, of which 8 were waited for; matrix products, arithmetic and copies ran while one was open for 33% of the time, Pallas kernels for 0%

commit v1 on v0

v1 whole, which is shorter than its diff:
```python
import functools

import jax
import jax.numpy as jnp
import numpy as np
from jax import lax
from jax.experimental import pallas as pl
from jax.experimental.pallas import tpu as pltpu
from jax.sharding import PartitionSpec as P

NCLASS = 4
PER = 10
COMPONENTS = 9
CHUNKS = ((0, 4), (4, 9))
MESH = pl.DeviceIdType.MESH


def block_tables():
    degree_list = []
    for block_number in range(8):
        for level in (block_number, 15 - block_number, 16 + block_number, 31 - block_number):
            for order in range(-level, level + 1):
                degree_list.append((level, order))
    order_list = []
    for block_number in range(8):
        if block_number == 0:
            magnitudes = (0, 16, 8, 24)
        else:
            magnitudes = (block_number, 32 - block_number, 16 - block_number, 16 + block_number)
        for size_m in magnitudes:
            for order in [size_m] if size_m == 0 else [size_m, -size_m]:
                for level in range(size_m, 32):
                    order_list.append((level, order))
    where_degree = {pair: index for index, pair in enumerate(degree_list)}
    by_degree = np.zeros((8, 128, 128), np.float32)
    by_order = np.zeros((8, 128, 128), np.float32)
    filled = np.zeros((8, 8), np.int32)
    for order_at, pair in enumerate(order_list):
        degree_at = where_degree[pair]
        a, b = degree_at // 128, order_at // 128
        slot = filled[a, b]
        filled[a, b] += 1
        by_degree[a, b * 16 + slot, degree_at % 128] = 1.0
        by_order[b, a * 16 + slot, order_at % 128] = 1.0
    assert (filled == 16).all()
    levels = np.array([pair[0] for pair in degree_list]).reshape(8, 128)
    orders = np.array([pair[1] for pair in order_list]).reshape(8, 128)
    same_level = (levels[:, :, None] == levels[:, None, :]).astype(np.float32)
    same_order = (orders[:, :, None] == orders[:, None, :]).astype(np.float32)
    return np.stack([by_degree, by_order, same_level, same_order], axis=1)


def pairs_of(first, last):
    return [tuple(range(s, min(s + 2, last))) for s in range(first, last, 2)]


def nt(left, right):
    return lax.dot_general(left, right, (((1,), (1,)), ((), ())), preferred_element_type=jnp.float32)


def nn(left, right):
    return jnp.dot(left, right, preferred_element_type=jnp.float32)


def kernel(x_ref, tables_hbm, rot_hbm, coax_hbm, offs_ref, cls_ref, out_ref, *scratch):
    count = len(CHUNKS)
    turned = scratch[0:count]
    got = scratch[count:2 * count]
    below = scratch[2 * count:3 * count]
    above = scratch[3 * count:4 * count]
    moved = scratch[4 * count:5 * count]
    back = scratch[5 * count:6 * count]
    (cells, tables, rot, coax, turning, turning_t, steps, chosen,
     load_sem, fwd_send, fwd_recv, halo_send, halo_recv, bwd_send, bwd_recv) = scratch[6 * count:]
    cell = lax.axis_index("cell")
    coef = lax.axis_index("coef")
    cell_total = lax.axis_size("cell")
    part = cell % 4
    plane = cell - part
    me = part * 8 + coef
    up = (cell + 4) % cell_total
    down = (cell + cell_total - 4) % cell_total

    def partner(i):
        other = (me + i) % 32
        return other, (plane + other // 8, other % 8)

    barrier = pltpu.get_barrier_semaphore()

    def greet(i, carry):
        pl.semaphore_signal(barrier, inc=1, device_id=partner(i)[1], device_id_type=MESH)
        return carry

    lax.fori_loop(1, 32, greet, 0)
    pl.semaphore_signal(barrier, inc=1, device_id=(up, coef), device_id_type=MESH)
    pl.semaphore_signal(barrier, inc=1, device_id=(down, coef), device_id_type=MESH)

    loads = [
        pltpu.make_async_copy(tables_hbm.at[coef], tables, load_sem.at[0]),
        pltpu.make_async_copy(rot_hbm, rot, load_sem.at[1]),
        pltpu.make_async_copy(coax_hbm, coax, load_sem.at[2]),
    ]
    for load in loads:
        load.start()
    loads[0].wait()
    loads[1].wait()
    for c in range(NCLASS):
        masked = rot[c, 0] * tables[2]
        turning[pl.ds(c * 128, 128), :] = nn(tables[0], masked).astype(jnp.bfloat16)

    def spread(source, target, send_sem, recv_sem):
        def one(i, carry):
            other, device = partner(i)
            pltpu.make_async_remote_copy(
                source.at[other], target.at[me], send_sem, recv_sem,
                device_id=device, device_id_type=MESH).start()
            return carry

        lax.fori_loop(1, 32, one, 0)
        pltpu.make_async_copy(source.at[me], target.at[me], recv_sem).start()

    for g, (first, last) in enumerate(CHUNKS):
        rows = x_ref[first:last].reshape((last - first) * 64, 128)
        result = nt(turning[...], rows).astype(jnp.bfloat16)
        turned[g][...] = result.reshape(32, 16, (last - first) * 64)
        if g == 0:
            pl.semaphore_wait(barrier, 33)
        spread(turned[g], got[g], fwd_send.at[g], fwd_recv.at[g])

    def pick(k, carry):
        seen, kept = carry[0], carry[1:]
        hit = cls_ref[k] == part
        kept = tuple(
            jnp.where(jnp.logical_and(hit, seen == p), k, old) for p, old in enumerate(kept))
        return (seen + jnp.where(hit, 1, 0),) + kept

    picked = lax.fori_loop(0, NCLASS * PER, pick, (jnp.int32(0),) * (PER + 1))[1:]
    for p in range(PER):
        chosen[p] = picked[p]
    loads[2].wait()

    def prepare(p, carry):
        masked = coax[chosen[p], 0] * tables[3]
        half = nn(tables[1], masked).astype(jnp.bfloat16)
        steps[p] = nt(half, tables[1]).astype(jnp.bfloat16)
        return carry

    lax.fori_loop(0, PER, prepare, 0)
    for c in range(NCLASS):
        piece = turning[pl.ds(c * 128, 128), :].astype(jnp.float32)
        turning_t[:, c * 128:(c + 1) * 128] = piece.T.astype(jnp.bfloat16)

    def lay(buffer, row, groups, g):
        first, last = CHUNKS[g]
        for j in range(groups):
            block = buffer[j * 8:(j + 1) * 8].reshape(128, (last - first) * 64)
            for at, s in enumerate(range(first, last, 2)):
                n = min(2, last - s)
                piece = block[:, at * 128:at * 128 + n * 64].astype(jnp.float32).T
                for m in range(n):
                    cells[s + m, row + j * 64:row + j * 64 + 64, :] = piece[m * 64:(m + 1) * 64]

    def arrive(g):
        pltpu.make_async_copy(got[g], got[g], fwd_recv.at[g]).wait()
        pltpu.make_async_remote_copy(
            got[g].at[pl.ds(16, 16)], below[g], halo_send.at[g, 0], halo_recv.at[g, 0],
            device_id=(up, coef), device_id_type=MESH).start()
        pltpu.make_async_remote_copy(
            got[g].at[pl.ds(0, 16)], above[g], halo_send.at[g, 1], halo_recv.at[g, 1],
            device_id=(down, coef), device_id_type=MESH).start()
        lay(got[g], 128, 4, g)

    def translate(g):
        first, last = CHUNKS[g]
        pltpu.make_async_copy(below[g], below[g], halo_recv.at[g, 0]).wait()
        lay(below[g], 0, 2, g)
        pltpu.make_async_copy(above[g], above[g], halo_recv.at[g, 1]).wait()
        lay(above[g], 384, 2, g)
        matrices = jnp.concatenate([steps[p] for p in range(PER)], axis=1)
        starts = [128 + offs_ref[chosen[p]] for p in range(PER)]
        for at, members in enumerate(pairs_of(first, last)):
            width = 64 * len(members)
            for j in range(0, 4, 2):
                pieces = []
                for p in range(PER):
                    pieces.append(jnp.concatenate(
                        [cells[s, pl.ds(starts[p] + i * 64, 64), :] for i in (j, j + 1) for s in members],
                        axis=0).astype(jnp.bfloat16))
                result = nt(matrices, jnp.concatenate(pieces, axis=1)).astype(jnp.bfloat16)
                for i in range(2):
                    moved[g][(j + i) * 8:(j + i + 1) * 8, :, at * 128:at * 128 + width] = (
                        result[:, i * width:(i + 1) * width].reshape(8, 16, width))
        spread(moved[g], back[g], bwd_send.at[g], bwd_recv.at[g])

    for g in range(count + 1):
        if g < count:
            arrive(g)
        if g > 0:
            translate(g - 1)

    for g, (first, last) in enumerate(CHUNKS):
        pltpu.make_async_copy(back[g], back[g], bwd_recv.at[g]).wait()
        block = back[g][...].reshape(512, (last - first) * 64)
        field = nn(turning_t[...], block)
        for at, members in enumerate(pairs_of(first, last)):
            piece = field[:, at * 128:at * 128 + 64 * len(members)].T.astype(jnp.bfloat16)
            for m, s in enumerate(members):
                out_ref[s] = piece[m * 64:(m + 1) * 64]

    for g in range(count):
        sent = turned[g].at[pl.ds(0, 31)]
        pltpu.make_async_copy(sent, sent, fwd_send.at[g]).wait()
        pltpu.make_async_copy(below[g], below[g], halo_send.at[g, 0]).wait()
        pltpu.make_async_copy(above[g], above[g], halo_send.at[g, 1]).wait()
        sent = moved[g].at[pl.ds(0, 31)]
        pltpu.make_async_copy(sent, sent, bwd_send.at[g]).wait()


def on_device(multipoles, rotation, coaxial, offsets, class_index):
    tables = jnp.asarray(block_tables(), jnp.bfloat16)
    rows = jnp.transpose(multipoles, (1, 0, 2))
    vmem = pl.BlockSpec(memory_space=pltpu.VMEM)
    smem = pl.BlockSpec(memory_space=pltpu.SMEM)
    hbm = pl.BlockSpec(memory_space=pl.ANY)
    count = len(CHUNKS)
    widths = [64 * (last - first) for first, last in CHUNKS]
    bf16 = jnp.bfloat16
    scratch = []
    for parts in (32, 32, 16, 16, 32, 32):
        scratch += [pltpu.VMEM((parts, 16, width), bf16) for width in widths]
    scratch += [
        pltpu.VMEM((COMPONENTS, 512, 128), jnp.float32),
        pltpu.VMEM((4, 128, 128), bf16),
        pltpu.VMEM((NCLASS, 1, 128, 128), bf16),
        pltpu.VMEM((NCLASS * PER, 1, 128, 128), bf16),
        pltpu.VMEM((NCLASS * 128, 128), bf16),
        pltpu.VMEM((128, NCLASS * 128), bf16),
        pltpu.VMEM((PER, 128, 128), bf16),
        pltpu.SMEM((PER,), jnp.int32),
        pltpu.SemaphoreType.DMA((3,)),
        pltpu.SemaphoreType.DMA((count,)),
        pltpu.SemaphoreType.DMA((count,)),
        pltpu.SemaphoreType.DMA((count, 2)),
        pltpu.SemaphoreType.DMA((count, 2)),
        pltpu.SemaphoreType.DMA((count,)),
        pltpu.SemaphoreType.DMA((count,)),
    ]
    field = pl.pallas_call(
        kernel,
        out_shape=jax.ShapeDtypeStruct((COMPONENTS, 64, 128), bf16),
        in_specs=[vmem, hbm, hbm, hbm, smem, smem],
        out_specs=vmem,
        scratch_shapes=scratch,
        compiler_params=pltpu.CompilerParams(collective_id=0, has_side_effects=True),
        name="multipole_to_local",
    )(rows, tables, rotation, coaxial, offsets, class_index)
    return jnp.transpose(field, (1, 0, 2))


def solution(mesh):
    placed = (
        P("cell", None, "coef"),
        P(None, "coef", None, None),
        P(None, "coef", None, None),
        P(),
        P(),
    )
    return jax.shard_map(
        on_device, mesh=mesh, in_specs=placed, out_specs=P("cell", None, "coef"), check_vma=False
    )
```

time: 502 us -> 45.1 us (0.09)
  the two profiles are of different devices: /device:TPU:2 before, /device:TPU:1 now
where the time goes in v1:
time: 45.1 us; the launch traced here: 44.9 us
  Pallas kernels  43.3 us (96%)
  local copies, waits for them, and re-layouts  1.58 us (4%)
    pallas_call x1, Pallas kernels, on_device(): pl.pallas_call(kernel, out_shape=jax.ShapeDtypeStruct((COMPONENTS, 64, 12...  43.3 us
    unnamed x1, local copies, waits for them, and re-layouts  1.58 us

profile of v1, /device:TPU:1, one launch (start us, length us, event | category | flops | bytes accessed | tf_op | source)
XLA Modules:
  0.0 44.9 jit_solution(6081737060169851682)
XLA Ops:
  0.0 43.3 %multipole_to_local.1 = bf16[9,64,128]{2,1,0:T(8,128)(2,1)} custom-call(bf16[9,64,128]{2,1,0:T(8,128)(2,1)} %bitcast.3, bf16[8,4,128,128]{3,2,1,0:T(8,128)(2,1)} %constant.2.clone.tables_hbm, bf16[4,1,128,128]{3,2,1,0:T(8,128)(2,1)} %rot_hbm.1, bf16[40,1,128,128]{3,2,1,0:T(8,128)(2,1)} %coax_hbm.1, s32[40]{0:T(128)} %offs_ref.1, s32[40]{0:T(128)} %cls_ref.1), custom_call_target="tpu_custom_call" | custom-call | tf_op jit(solution)/shard_map/multipole_to_local/pallas_call | solution.py:248
  43.3 1.6 %copy.8 = bf16[64,9,128]{2,0,1:T(8,128)(2,1)} copy(bf16[64,9,128]{2,0,1:T(8,128)(2,1)} %bitcast.2) | data formatting | bytes 294912

commit v2 on v1

v2 whole, which is shorter than its diff:
```python
import jax
import jax.numpy as jnp
import numpy as np
from jax import lax
from jax.experimental import pallas as pl
from jax.experimental.pallas import tpu as pltpu
from jax.sharding import PartitionSpec as P

NCLASS = 4
PER = 10
COMPONENTS = 9
CHUNKS = ((0, 2), (2, 4), (4, 6), (6, 8), (8, 9))
MESH = pl.DeviceIdType.MESH


def block_tables():
    degree_list = []
    for block_number in range(8):
        for level in (block_number, 15 - block_number, 16 + block_number, 31 - block_number):
            for order in range(-level, level + 1):
                degree_list.append((level, order))
    order_list = []
    for block_number in range(8):
        if block_number == 0:
            magnitudes = (0, 16, 8, 24)
        else:
            magnitudes = (block_number, 32 - block_number, 16 - block_number, 16 + block_number)
        for size_m in magnitudes:
            for order in [size_m] if size_m == 0 else [size_m, -size_m]:
                for level in range(size_m, 32):
                    order_list.append((level, order))
    where_degree = {pair: index for index, pair in enumerate(degree_list)}
    by_degree = np.zeros((8, 128, 128), np.float32)
    by_order = np.zeros((8, 128, 128), np.float32)
    filled = np.zeros((8, 8), np.int32)
    for order_at, pair in enumerate(order_list):
        degree_at = where_degree[pair]
        a, b = degree_at // 128, order_at // 128
        slot = filled[a, b]
        filled[a, b] += 1
        by_degree[a, b * 16 + slot, degree_at % 128] = 1.0
        by_order[b, (slot // 8) * 64 + a * 8 + slot % 8, order_at % 128] = 1.0
    assert (filled == 16).all()
    levels = np.array([pair[0] for pair in degree_list]).reshape(8, 128)
    orders = np.array([pair[1] for pair in order_list]).reshape(8, 128)
    same_level = (levels[:, :, None] == levels[:, None, :]).astype(np.float32)
    same_order = (orders[:, :, None] == orders[:, None, :]).astype(np.float32)
    return np.stack([by_degree, by_order, same_level, same_order], axis=1)


def packed(g):
    return CHUNKS[g][1] - CHUNKS[g][0] == 1


def depth(g):
    return 8 if packed(g) else 16


def lanes(g):
    return max(128, 64 * (CHUNKS[g][1] - CHUNKS[g][0]))


def nt(left, right):
    return lax.dot_general(left, right, (((1,), (1,)), ((), ())), preferred_element_type=jnp.float32)


def nn(left, right):
    return jnp.dot(left, right, preferred_element_type=jnp.float32)


def halves_first(rows):
    count, width = rows.shape[0] // 16, rows.shape[1]
    split = rows.reshape(count, 2, 8, width)
    return jnp.concatenate([split[:, h].reshape(count * 8, width) for h in range(2)], axis=0)


def halves_last(rows):
    count, width = rows.shape[0] // 16, rows.shape[1]
    split = rows.reshape(2, count, 8, width)
    pieces = [split[h, n] for n in range(count) for h in range(2)]
    return jnp.concatenate(pieces, axis=0)


def kernel(x_hbm, tables_hbm, rot_hbm, coax_hbm, offs_ref, cls_ref, out_ref, *scratch):
    count = len(CHUNKS)
    names = ("turned", "middle", "got", "below", "above", "moved", "between", "back")
    buffers = {name: scratch[i * count:(i + 1) * count] for i, name in enumerate(names)}
    turned, middle, got, below, above, moved, between, back = (buffers[name] for name in names)
    (x_ref, cells, tables, rot, coax, turning, turning_t, steps, chosen, load_sem,
     fx_send, fx_recv, fy_send, fy_recv, halo_send, halo_recv,
     bx_send, bx_recv, by_send, by_recv) = scratch[len(names) * count:]
    cell = lax.axis_index("cell")
    coef = lax.axis_index("coef")
    cell_total = lax.axis_size("cell")
    part = cell % 4
    plane = cell - part
    along = coef % 4
    high = coef // 4
    column = part * 2 + high
    up = (cell + 4) % cell_total
    down = (cell + cell_total - 4) % cell_total

    def along_device(i):
        other = (along + i) % 4
        return other, (cell, high * 4 + other)

    def column_device(i):
        other = (column + i) % 8
        return other, (plane + other // 2, (other % 2) * 4 + along)

    def half_device(half, i):
        other = half * 4 + (column + i) % 4
        return other, (plane + other // 2, (other % 2) * 4 + along)

    barrier = pltpu.get_barrier_semaphore()
    friends = [along_device(i)[1] for i in range(1, 4)] + [column_device(i)[1] for i in range(1, 8)]
    friends += [(up, coef), (down, coef)]
    for device in friends:
        pl.semaphore_signal(barrier, inc=1, device_id=device, device_id_type=MESH)

    loads = [
        pltpu.make_async_copy(tables_hbm.at[coef], tables, load_sem.at[0]),
        pltpu.make_async_copy(rot_hbm, rot, load_sem.at[1]),
        pltpu.make_async_copy(coax_hbm, coax, load_sem.at[2]),
        pltpu.make_async_copy(x_hbm, x_ref, load_sem.at[3]),
    ]
    for load in (loads[0], loads[1], loads[3], loads[2]):
        load.start()
    loads[0].wait()
    loads[1].wait()
    for c in range(NCLASS):
        masked = rot[c, 0] * tables[2]
        rows = nn(tables[0], masked).astype(jnp.bfloat16)
        for b in range(8):
            at = ((b % 4) * 8 + c * 2 + b // 4) * 16
            turning[at:at + 16, :] = rows[b * 16:(b + 1) * 16]

    def send(source, target, send_sem, recv_sem, device):
        pltpu.make_async_remote_copy(
            source, target, send_sem, recv_sem, device_id=device, device_id_type=MESH).start()

    def landed(ref, sem):
        pltpu.make_async_copy(ref, ref, sem).wait()

    loads[3].wait()
    for g, (first, last) in enumerate(CHUNKS):
        rows = x_ref[first:last].reshape((last - first) * 64, 128)
        if packed(g):
            matrix = halves_first(turning[...].astype(jnp.float32)).astype(jnp.bfloat16)
            result = nt(matrix, rows)
            result = jnp.concatenate([result[:256], result[256:]], axis=1)
        else:
            result = nt(turning[...], rows)
        turned[g][...] = result.astype(jnp.bfloat16).reshape(4, 8, depth(g), lanes(g))
        if g == 0:
            pl.semaphore_wait(barrier, len(friends))
        for i in range(1, 4):
            other, device = along_device(i)
            send(turned[g].at[other], middle[g].at[:, along], fx_send.at[g], fx_recv.at[g], device)
        pltpu.make_async_copy(
            turned[g].at[along], middle[g].at[:, along], fx_recv.at[g]).start()

    def pick(k, carry):
        seen, kept = carry[0], carry[1:]
        hit = cls_ref[k] == part
        kept = tuple(
            jnp.where(jnp.logical_and(hit, seen == p), k, old) for p, old in enumerate(kept))
        return (seen + jnp.where(hit, 1, 0),) + kept

    def forward(g):
        landed(middle[g], fx_recv.at[g])
        for i in range(1, 8):
            other, device = column_device(i)
            send(middle[g].at[other], got[g].at[column], fy_send.at[g], fy_recv.at[g], device)
        pltpu.make_async_copy(
            middle[g].at[column], got[g].at[column], fy_recv.at[g]).start()

    def prepare_steps():
        picked = lax.fori_loop(0, NCLASS * PER, pick, (jnp.int32(0),) * (PER + 1))[1:]
        for p in range(PER):
            chosen[p] = picked[p]
        loads[2].wait()

        def prepare(p, carry):
            masked = coax[chosen[p], 0] * tables[3]
            half = nn(tables[1], masked).astype(jnp.bfloat16)
            steps[p] = nt(half, tables[1]).astype(jnp.bfloat16)
            return carry

        lax.fori_loop(0, PER, prepare, 0)

    def prepare_return():
        pieces = []
        for c in range(NCLASS):
            for b in range(8):
                at = ((b % 4) * 8 + c * 2 + b // 4) * 16
                pieces.append(turning[at:at + 16, :])
        rows = jnp.concatenate(pieces, axis=0).astype(jnp.float32)
        for kind, matrix in enumerate((rows, halves_first(rows))):
            for c in range(NCLASS):
                turning_t[kind, :, c * 128:(c + 1) * 128] = (
                    matrix[c * 128:(c + 1) * 128].T.astype(jnp.bfloat16))

    def lay(buffer, row, groups, g):
        first, last = CHUNKS[g]
        for j in range(groups):
            block = buffer[j * 2:(j + 1) * 2].reshape(8 * depth(g), lanes(g))
            if packed(g):
                piece = block.astype(jnp.float32).T
                cells[first, row + j * 64:row + j * 64 + 64, :] = jnp.concatenate(
                    [piece[:64], piece[64:]], axis=1)
                continue
            for at in range(0, lanes(g), 128):
                piece = halves_first(block[:, at:at + 128].astype(jnp.float32)).T
                for m in range(2):
                    cells[first + at // 64 + m, row + j * 64:row + j * 64 + 64, :] = (
                        piece[m * 64:(m + 1) * 64])

    def arrive(g):
        landed(got[g], fy_recv.at[g])
        send(got[g].at[pl.ds(0, 4)], above[g], halo_send.at[g, 1], halo_recv.at[g, 1], (down, coef))
        send(got[g].at[pl.ds(4, 4)], below[g], halo_send.at[g, 0], halo_recv.at[g, 0], (up, coef))
        lay(got[g], 128, 4, g)

    def translate(g, half):
        first, last = CHUNKS[g]
        if half:
            landed(above[g], halo_recv.at[g, 1])
            lay(above[g], 384, 2, g)
        else:
            landed(below[g], halo_recv.at[g, 0])
            lay(below[g], 0, 2, g)
        matrices = jnp.concatenate([steps[p] for p in range(PER)], axis=1)
        starts = [128 + half * 128 + offs_ref[chosen[p]] for p in range(PER)]
        for at, s0 in enumerate(range(first, last, 2)):
            members = range(s0, min(s0 + 2, last))
            width = 64 * len(members)
            pieces = []
            for p in range(PER):
                pieces.append(jnp.concatenate(
                    [cells[s, pl.ds(starts[p] + i * 64, 64), :] for i in range(2) for s in members],
                    axis=0).astype(jnp.bfloat16))
            result = nt(matrices, jnp.concatenate(pieces, axis=1))
            for i in range(2):
                piece = result[:, i * width:(i + 1) * width]
                if packed(g):
                    piece = jnp.concatenate([piece[:64], piece[64:]], axis=1)
                else:
                    piece = halves_last(piece)
                piece = piece.astype(jnp.bfloat16).reshape(8, depth(g), 128)
                for a in range(8):
                    moved[g][a % 4, (half * 2 + i) * 2 + a // 4, :, at * 128:at * 128 + 128] = piece[a]
        span = pl.ds(half * 4, 4)
        for i in range(1, 4):
            other, device = along_device(i)
            send(moved[g].at[other, span], between[g].at[span, along],
                 bx_send.at[g, half], bx_recv.at[g, half], device)
        pltpu.make_async_copy(
            moved[g].at[along, span], between[g].at[span, along], bx_recv.at[g, half]).start()

    def onward(g, half):
        landed(between[g].at[pl.ds(half * 4, 4)], bx_recv.at[g, half])
        inside = column // 4 == half
        for i in range(4):
            other, device = half_device(half, i)
            if i:
                send(between[g].at[other], back[g].at[column], by_send.at[g, half], by_recv.at[g], device)
            else:
                @pl.when(jnp.logical_not(inside))
                def _():
                    send(between[g].at[other], back[g].at[column], by_send.at[g, half], by_recv.at[g], device)

                @pl.when(inside)
                def _():
                    pltpu.make_async_copy(
                        between[g].at[other], back[g].at[column], by_recv.at[g]).start()

    def finish(g):
        first, last = CHUNKS[g]
        landed(back[g], by_recv.at[g])
        block = back[g][...].reshape(32 * depth(g), lanes(g))
        if packed(g):
            block = jnp.concatenate([block[:, :64], block[:, 64:]], axis=0)
        matrix = turning_t[1 if packed(g) else 0]
        field = nn(matrix, block)
        for at, s0 in enumerate(range(first, last, 2)):
            members = range(s0, min(s0 + 2, last))
            piece = field[:, at * 128:at * 128 + 64 * len(members)].T.astype(jnp.bfloat16)
            for m, s in enumerate(members):
                out_ref[s] = piece[m * 64:(m + 1) * 64]

    forward(0)
    prepare_steps()
    prepare_return()
    for g in range(1, count + 2):
        if g < count:
            forward(g)
        if g - 1 < count:
            arrive(g - 1)
        if g >= 2:
            translate(g - 2, 1)
    onward(0, 1)
    for g in range(count):
        translate(g, 0)
        if g + 1 < count:
            onward(g + 1, 1)
        if g:
            onward(g - 1, 0)
    onward(count - 1, 0)
    for g in range(count):
        finish(g)

    for g in range(count):
        landed(turned[g].at[pl.ds(0, 3)], fx_send.at[g])
        landed(middle[g].at[pl.ds(0, 7)], fy_send.at[g])
        landed(below[g], halo_send.at[g, 0])
        landed(above[g], halo_send.at[g, 1])
        for half in range(2):
            landed(moved[g].at[pl.ds(0, 3), pl.ds(0, 4)], bx_send.at[g, half])

            @pl.when(column // 4 == half)
            def _():
                landed(between[g].at[pl.ds(0, 3)], by_send.at[g, half])

            @pl.when(column // 4 != half)
            def _():
                landed(between[g].at[pl.ds(0, 4)], by_send.at[g, half])


def on_device(multipoles, rotation, coaxial, offsets, class_index):
    tables = jnp.asarray(block_tables(), jnp.bfloat16)
    rows = jnp.transpose(multipoles, (1, 0, 2))
    vmem = pl.BlockSpec(memory_space=pltpu.VMEM)
    smem = pl.BlockSpec(memory_space=pltpu.SMEM)
    hbm = pl.BlockSpec(memory_space=pl.ANY)
    count = len(CHUNKS)
    bf16 = jnp.bfloat16
    scratch = []
    for outer in ((4, 8), (8, 4), (8, 4), (4, 4), (4, 4), (4, 8), (8, 4), (8, 4)):
        scratch += [pltpu.VMEM(outer + (depth(g), lanes(g)), bf16) for g in range(count)]
    dma = pltpu.SemaphoreType.DMA
    scratch += [
        pltpu.VMEM((COMPONENTS, 64, 128), bf16),
        pltpu.VMEM((COMPONENTS, 512, 128), jnp.float32),
        pltpu.VMEM((4, 128, 128), bf16),
        pltpu.VMEM((NCLASS, 1, 128, 128), bf16),
        pltpu.VMEM((NCLASS * PER, 1, 128, 128), bf16),
        pltpu.VMEM((NCLASS * 128, 128), bf16),
        pltpu.VMEM((2, 128, NCLASS * 128), bf16),
        pltpu.VMEM((PER, 128, 128), bf16),
        pltpu.SMEM((PER,), jnp.int32),
        dma((4,)),
        dma((count,)), dma((count,)), dma((count,)), dma((count,)),
        dma((count, 2)), dma((count, 2)),
        dma((count, 2)), dma((count, 2)), dma((count, 2)), dma((count,)),
    ]
    field = pl.pallas_call(
        kernel,
        out_shape=jax.ShapeDtypeStruct((COMPONENTS, 64, 128), bf16),
        in_specs=[hbm, hbm, hbm, hbm, smem, smem],
        out_specs=vmem,
        scratch_shapes=scratch,
        compiler_params=pltpu.CompilerParams(collective_id=0, has_side_effects=True),
        name="multipole_to_local",
    )(rows, tables, rotation, coaxial, offsets, class_index)
    return jnp.transpose(field, (1, 0, 2))


def solution(mesh):
    placed = (
        P("cell", None, "coef"),
        P(None, "coef", None, None),
        P(None, "coef", None, None),
        P(),
        P(),
    )
    return jax.shard_map(
        on_device, mesh=mesh, in_specs=placed, out_specs=P("cell", None, "coef"), check_vma=False
    )
```

time: 45.1 us -> 52.7 us (1.17)
  Pallas kernels: 43.3 us -> 50.9 us
    pallas_call x1, Pallas kernels: 43.3 us -> 50.9 us  [on_device(): pl.pallas_call(kernel, out_shape=jax.ShapeDtypeStruct((COMPONENTS, 64, 12...]
where the time goes in v2:
time: 52.7 us; the launch traced here: 52.5 us
  Pallas kernels  50.9 us (97%)
  local copies, waits for them, and re-layouts  1.58 us (3%)
    pallas_call x1, Pallas kernels, on_device(): pl.pallas_call(kernel, out_shape=jax.ShapeDtypeStruct((COMPONENTS, 64, 12...  50.9 us
    unnamed x1, local copies, waits for them, and re-layouts  1.58 us

profile of v2, /device:TPU:1, one launch (start us, length us, event | category | flops | bytes accessed | tf_op | source)
XLA Modules:
  0.0 52.5 jit_solution(16125286277111670441)
XLA Ops:
  0.0 50.9 %multipole_to_local.1 = bf16[9,64,128]{2,1,0:T(8,128)(2,1)} custom-call(bf16[9,64,128]{2,1,0:T(8,128)(2,1)} %bitcast.3, bf16[8,4,128,128]{3,2,1,0:T(8,128)(2,1)} %constant.2.clone.tables_hbm, bf16[4,1,128,128]{3,2,1,0:T(8,128)(2,1)} %rot_hbm.1, bf16[40,1,128,128]{3,2,1,0:T(8,128)(2,1)} %coax_hbm.1, s32[40]{0:T(128)} %offs_ref.1, s32[40]{0:T(128)} %cls_ref.1), custom_call_target="tpu_custom_call" | custom-call | tf_op jit(solution)/shard_map/multipole_to_local/pallas_call | solution.py:357
  50.9 1.6 %copy.8 = bf16[64,9,128]{2,0,1:T(8,128)(2,1)} copy(bf16[64,9,128]{2,0,1:T(8,128)(2,1)} %bitcast.2) | data formatting | bytes 294912

commit v3 on v2

v3 whole, which is shorter than its diff:
```python
import jax
import jax.numpy as jnp
import numpy as np
from jax import lax
from jax.experimental import pallas as pl
from jax.experimental.pallas import tpu as pltpu
from jax.sharding import PartitionSpec as P

NCLASS = 4
PER = 10
COMPONENTS = 9
CHUNKS = ((0, 4), (4, 9))
ORDER = ("a0", "h0", "a1", "h1", "l0", "l1", "e0", "e1")
MESH = pl.DeviceIdType.MESH


def far_first():
    ways = {}
    for dx in range(4):
        for dy in range(4):
            for dc in range(2):
                if (dx, dy, dc) != (0, 0, 0):
                    ways.setdefault((dx, dy), []).append((dx, dy, dc))
    hops = lambda way: min(way[0], 4 - way[0]) + min(way[1], 4 - way[1])
    keys = sorted(ways, key=lambda way: -hops(way))
    return [ways[key][-1 - turn] for turn in range(2) for key in keys if turn < len(ways[key])]


FAR_FIRST = far_first()
HALF_FAR_FIRST = [
    (dx, dh, dc) for dc in (1, 0) for dx, dh in (
        (2, 1), (2, 0), (1, 1), (3, 1), (0, 1), (1, 0), (3, 0), (0, 0))]


def block_tables():
    degree_list = []
    for block_number in range(8):
        for level in (block_number, 15 - block_number, 16 + block_number, 31 - block_number):
            for order in range(-level, level + 1):
                degree_list.append((level, order))
    order_list = []
    for block_number in range(8):
        if block_number == 0:
            magnitudes = (0, 16, 8, 24)
        else:
            magnitudes = (block_number, 32 - block_number, 16 - block_number, 16 + block_number)
        for size_m in magnitudes:
            for order in [size_m] if size_m == 0 else [size_m, -size_m]:
                for level in range(size_m, 32):
                    order_list.append((level, order))
    where_degree = {pair: index for index, pair in enumerate(degree_list)}
    by_degree = np.zeros((8, 128, 128), np.float32)
    by_order = np.zeros((8, 128, 128), np.float32)
    filled = np.zeros((8, 8), np.int32)
    for order_at, pair in enumerate(order_list):
        degree_at = where_degree[pair]
        a, b = degree_at // 128, order_at // 128
        slot = filled[a, b]
        filled[a, b] += 1
        by_degree[a, b * 16 + slot, degree_at % 128] = 1.0
        by_order[b, (slot // 8) * 64 + a * 8 + slot % 8, order_at % 128] = 1.0
    assert (filled == 16).all()
    levels = np.array([pair[0] for pair in degree_list]).reshape(8, 128)
    orders = np.array([pair[1] for pair in order_list]).reshape(8, 128)
    same_level = (levels[:, :, None] == levels[:, None, :]).astype(np.float32)
    same_order = (orders[:, :, None] == orders[:, None, :]).astype(np.float32)
    return np.stack([by_degree, by_order, same_level, same_order], axis=1)


def tiles(g):
    return CHUNKS[g][1] - CHUNKS[g][0]


def nt(left, right):
    return lax.dot_general(left, right, (((1,), (1,)), ((), ())), preferred_element_type=jnp.float32)


def nn(left, right):
    return jnp.dot(left, right, preferred_element_type=jnp.float32)


def halves_first(rows):
    count, width = rows.shape[0] // 16, rows.shape[1]
    split = rows.reshape(count, 2, 8, width)
    return jnp.concatenate([split[:, h].reshape(count * 8, width) for h in range(2)], axis=0)


def kernel(x_hbm, tables_hbm, rot_hbm, coax_hbm, offs_ref, cls_ref, out_ref, *scratch):
    count = len(CHUNKS)
    names = ("turned", "got", "below", "above", "moved", "back")
    buffers = {name: scratch[i * count:(i + 1) * count] for i, name in enumerate(names)}
    turned, got, below, above, moved, back = (buffers[name] for name in names)
    (x_ref, cells, tables, rot, coax, turning, turning_t, steps, chosen, load_sem, late_sem,
     fwd_send, fwd_recv, halo_send, halo_recv, bwd_send, bwd_recv) = scratch[len(names) * count:]
    cell = lax.axis_index("cell")
    coef = lax.axis_index("coef")
    cell_total = lax.axis_size("cell")
    part = cell % 4
    plane = cell - part
    me = part * 8 + coef
    along, high, low, core = coef % 4, coef // 4, part // 2, part % 2
    up = (cell + 4) % cell_total
    down = (cell + cell_total - 4) % cell_total
    is_first = jnp.logical_and(cell == 0, coef == 0)
    beside_first = jnp.logical_and(coef == 0, jnp.logical_or(up == 0, down == 0))
    knows_first = jnp.logical_and(
        jnp.logical_not(is_first), jnp.logical_or(plane == 0, beside_first))

    xs = [(along + i) % 4 for i in range(4)]
    ys = [(high * 2 + low + i) % 4 for i in range(4)]
    cores = [core, 1 - core]

    def partner(dx, dy, dc):
        to_part = (ys[dy] % 2) * 2 + cores[dc]
        to_coef = (ys[dy] // 2) * 4 + xs[dx]
        return to_part * 8 + to_coef, (plane + to_part, to_coef)

    def half_partner(half, dx, dh, dc):
        to_part = half * 2 + cores[dc]
        to_coef = (high + dh) % 2 * 4 + xs[dx]
        return to_part * 8 + to_coef, (plane + to_part, to_coef)

    barrier = pltpu.get_barrier_semaphore()
    friends = [partner(*step)[1] for step in FAR_FIRST] + [(up, coef), (down, coef)]

    @pl.when(jnp.logical_not(is_first))
    def _():
        for device in friends:
            pl.semaphore_signal(barrier, inc=1, device_id=device, device_id_type=MESH)

    loads = [
        pltpu.make_async_copy(tables_hbm.at[coef], tables, load_sem.at[0]),
        pltpu.make_async_copy(rot_hbm, rot, load_sem.at[1]),
        pltpu.make_async_copy(coax_hbm, coax, load_sem.at[2]),
        pltpu.make_async_copy(x_hbm, x_ref, load_sem.at[3]),
    ]
    for load in (loads[0], loads[1], loads[3], loads[2]):
        load.start()

    @pl.when(is_first)
    def _():
        pl.semaphore_wait(barrier, len(friends))
        for device in friends:
            pl.semaphore_signal(late_sem, inc=1, device_id=device, device_id_type=MESH)

    loads[0].wait()
    loads[1].wait()
    for c in range(NCLASS):
        masked = rot[c, 0] * tables[2]
        turning[c * 128:(c + 1) * 128, :] = nn(tables[0], masked).astype(jnp.bfloat16)

    def send(source, target, send_sem, recv_sem, device):
        pltpu.make_async_remote_copy(
            source, target, send_sem, recv_sem, device_id=device, device_id_type=MESH).start()

    def landed(ref, sem):
        pltpu.make_async_copy(ref, ref, sem).wait()

    def turn(g):
        first, last = CHUNKS[g]
        for at, s0 in enumerate(range(first, last, 2)):
            members = range(s0, min(s0 + 2, last))
            rows = x_ref[s0:members[-1] + 1].reshape(len(members) * 64, 128)
            result = nt(turning[...], rows).reshape(32, 2, 8, len(members) * 64)
            if len(members) == 1:
                result = jnp.concatenate([result[:, 0], result[:, 1]], axis=2)
                turned[g][:, 2 * at] = result.astype(jnp.bfloat16)
            else:
                for h in range(2):
                    turned[g][:, 2 * at + h] = result[:, h].astype(jnp.bfloat16)

    def spread(g):
        for step in FAR_FIRST:
            other, device = partner(*step)

            @pl.when(jnp.logical_or(plane != 0, other != 0))
            def _():
                send(turned[g].at[other], got[g].at[me], fwd_send.at[g], fwd_recv.at[g], device)

        pltpu.make_async_copy(turned[g].at[me], got[g].at[me], fwd_recv.at[g]).start()

    def greet_first():
        @pl.when(knows_first)
        def _():
            pl.semaphore_wait(late_sem, 1)

        @pl.when(jnp.logical_and(knows_first, plane == 0))
        def _():
            for g in range(count):
                send(turned[g].at[0], got[g].at[me], fwd_send.at[g], fwd_recv.at[g], (0, 0))

    def pick(k, carry):
        seen, kept = carry[0], carry[1:]
        hit = cls_ref[k] == part
        kept = tuple(
            jnp.where(jnp.logical_and(hit, seen == p), k, old) for p, old in enumerate(kept))
        return (seen + jnp.where(hit, 1, 0),) + kept

    def prepare_steps():
        picked = lax.fori_loop(0, NCLASS * PER, pick, (jnp.int32(0),) * (PER + 1))[1:]
        for p in range(PER):
            chosen[p] = picked[p]
        loads[2].wait()

        def prepare(p, carry):
            masked = coax[chosen[p], 0] * tables[3]
            half = nn(tables[1], masked).astype(jnp.bfloat16)
            steps[p] = nt(half, tables[1]).astype(jnp.bfloat16)
            return carry

        lax.fori_loop(0, PER, prepare, 0)

    def prepare_return():
        rows = halves_first(turning[...].astype(jnp.float32))
        for c in range(NCLASS):
            turning_t[:, c * 128:(c + 1) * 128] = rows[c * 128:(c + 1) * 128].T.astype(jnp.bfloat16)

    def lay(buffer, row, groups, g):
        first, last = CHUNKS[g]
        for j in range(groups):
            for at, s0 in enumerate(range(first, last, 2)):
                if s0 + 1 == last:
                    block = buffer[j * 8:(j + 1) * 8, 2 * at].astype(jnp.float32).reshape(64, 128).T
                    cells[s0, row + j * 64:row + j * 64 + 64, :] = jnp.concatenate(
                        [block[:64], block[64:]], axis=1)
                    continue
                block = jnp.concatenate(
                    [buffer[j * 8:(j + 1) * 8, 2 * at + h].astype(jnp.float32).reshape(64, 128)
                     for h in range(2)], axis=0).T
                for m in range(2):
                    cells[s0 + m, row + j * 64:row + j * 64 + 64, :] = block[m * 64:(m + 1) * 64]

    def arrive(g):
        landed(got[g], fwd_recv.at[g])
        send(got[g].at[pl.ds(0, 16)], above[g], halo_send.at[g, 1], halo_recv.at[g, 1], (down, coef))
        send(got[g].at[pl.ds(16, 16)], below[g], halo_send.at[g, 0], halo_recv.at[g, 0], (up, coef))
        lay(got[g], 128, 4, g)

    def translate(g, half):
        first, last = CHUNKS[g]
        if half:
            landed(above[g], halo_recv.at[g, 1])
            lay(above[g], 384, 2, g)
        else:
            landed(below[g], halo_recv.at[g, 0])
            lay(below[g], 0, 2, g)
        matrices = jnp.concatenate([steps[p] for p in range(PER)], axis=1)
        starts = [128 + half * 128 + offs_ref[chosen[p]] for p in range(PER)]
        for at, s0 in enumerate(range(first, last, 2)):
            members = range(s0, min(s0 + 2, last))
            width = 64 * len(members)
            pieces = []
            for p in range(PER):
                pieces.append(jnp.concatenate(
                    [cells[s, pl.ds(starts[p] + i * 64, 64), :] for i in range(2) for s in members],
                    axis=0).astype(jnp.bfloat16))
            result = nt(matrices, jnp.concatenate(pieces, axis=1))
            for i in range(2):
                row = (half * 2 + i) * 8
                piece = result[:, i * width:(i + 1) * width]
                if len(members) == 1:
                    piece = jnp.concatenate([piece[:64], piece[64:]], axis=1)
                    moved[g][row:row + 8, 2 * at] = piece.reshape(8, 8, 128).astype(jnp.bfloat16)
                else:
                    for h in range(2):
                        moved[g][row:row + 8, 2 * at + h] = (
                            piece[h * 64:(h + 1) * 64].reshape(8, 8, 128).astype(jnp.bfloat16))
        for step in HALF_FAR_FIRST:
            other, device = half_partner(half, *step)
            if step == (0, 0, 0):
                @pl.when(low != half)
                def _():
                    send(moved[g].at[other], back[g].at[me], bwd_send.at[g, half], bwd_recv.at[g], device)

                @pl.when(low == half)
                def _():
                    pltpu.make_async_copy(moved[g].at[me], back[g].at[me], bwd_recv.at[g]).start()
            else:
                send(moved[g].at[other], back[g].at[me], bwd_send.at[g, half], bwd_recv.at[g], device)

    def finish(g):
        first, last = CHUNKS[g]
        landed(back[g], bwd_recv.at[g])
        matrix = turning_t[...]
        for at, s0 in enumerate(range(first, last, 2)):
            if s0 + 1 == last:
                block = back[g][:, 2 * at].reshape(256, 128)
                block = jnp.concatenate([block[:, :64], block[:, 64:]], axis=0)
                out_ref[s0] = nn(matrix, block).T.astype(jnp.bfloat16)
                continue
            block = jnp.concatenate([back[g][:, 2 * at + h].reshape(256, 128) for h in range(2)], axis=0)
            piece = nn(matrix, block).T.astype(jnp.bfloat16)
            for m in range(2):
                out_ref[s0 + m] = piece[m * 64:(m + 1) * 64]

    loads[3].wait()
    for g in range(count):
        turn(g)
        if g == 0:
            @pl.when(jnp.logical_not(is_first))
            def _():
                pl.semaphore_wait(barrier, len(friends) - jnp.where(knows_first, 1, 0))
        spread(g)
    prepare_steps()
    prepare_return()
    greet_first()
    stages = {
        "a": arrive, "h": lambda g: translate(g, 1), "l": lambda g: translate(g, 0), "e": finish,
    }
    for token in ORDER:
        stages[token[0]](int(token[1:]))

    for g in range(count):
        landed(turned[g].at[pl.ds(0, 31)], fwd_send.at[g])
        landed(below[g], halo_send.at[g, 0])
        landed(above[g], halo_send.at[g, 1])
        for half in range(2):
            @pl.when(low == half)
            def _():
                landed(moved[g].at[pl.ds(0, 15)], bwd_send.at[g, half])

            @pl.when(low != half)
            def _():
                landed(moved[g].at[pl.ds(0, 16)], bwd_send.at[g, half])


def on_device(multipoles, rotation, coaxial, offsets, class_index):
    tables = jnp.asarray(block_tables(), jnp.bfloat16)
    rows = jnp.transpose(multipoles, (1, 0, 2))
    vmem = pl.BlockSpec(memory_space=pltpu.VMEM)
    smem = pl.BlockSpec(memory_space=pltpu.SMEM)
    hbm = pl.BlockSpec(memory_space=pl.ANY)
    count = len(CHUNKS)
    bf16 = jnp.bfloat16
    scratch = []
    for outer in (32, 32, 16, 16, 32, 32):
        scratch += [pltpu.VMEM((outer, tiles(g), 8, 128), bf16) for g in range(count)]
    dma = pltpu.SemaphoreType.DMA
    scratch += [
        pltpu.VMEM((COMPONENTS, 64, 128), bf16),
        pltpu.VMEM((COMPONENTS, 512, 128), jnp.float32),
        pltpu.VMEM((4, 128, 128), bf16),
        pltpu.VMEM((NCLASS, 1, 128, 128), bf16),
        pltpu.VMEM((NCLASS * PER, 1, 128, 128), bf16),
        pltpu.VMEM((NCLASS * 128, 128), bf16),
        pltpu.VMEM((128, NCLASS * 128), bf16),
        pltpu.VMEM((PER, 128, 128), bf16),
        pltpu.SMEM((PER,), jnp.int32),
        dma((4,)), pltpu.SemaphoreType.REGULAR,
        dma((count,)), dma((count,)),
        dma((count, 2)), dma((count, 2)),
        dma((count, 2)), dma((count,)),
    ]
    field = pl.pallas_call(
        kernel,
        out_shape=jax.ShapeDtypeStruct((COMPONENTS, 64, 128), bf16),
        in_specs=[hbm, hbm, hbm, hbm, smem, smem],
        out_specs=vmem,
        scratch_shapes=scratch,
        compiler_params=pltpu.CompilerParams(collective_id=0, has_side_effects=True),
        name="multipole_to_local",
    )(rows, tables, rotation, coaxial, offsets, class_index)
    return jnp.transpose(field, (1, 0, 2))


def solution(mesh):
    placed = (
        P("cell", None, "coef"),
        P(None, "coef", None, None),
        P(None, "coef", None, None),
        P(),
        P(),
    )
    return jax.shard_map(
        on_device, mesh=mesh, in_specs=placed, out_specs=P("cell", None, "coef"), check_vma=False
    )
```

time: 52.7 us -> 41.1 us (0.78)
  Pallas kernels: 50.9 us -> 38.9 us
    pallas_call x1, Pallas kernels: 50.9 us -> 38.9 us  [on_device(): pl.pallas_call(kernel, out_shape=jax.ShapeDtypeStruct((COMPONENTS, 64, 12...]
where the time goes in v3:
time: 41.1 us; the launch traced here: 40.5 us
  Pallas kernels  38.9 us (95%)
  local copies, waits for them, and re-layouts  1.58 us (4%)
    pallas_call x1, Pallas kernels, on_device(): pl.pallas_call(kernel, out_shape=jax.ShapeDtypeStruct((COMPONENTS, 64, 12...  38.9 us
    unnamed x1, local copies, waits for them, and re-layouts  1.58 us

profile of v3, /device:TPU:1, one launch (start us, length us, event | category | flops | bytes accessed | tf_op | source)
XLA Modules:
  0.0 40.5 jit_solution(16065233353303882081)
XLA Ops:
  0.0 38.9 %multipole_to_local.1 = bf16[9,64,128]{2,1,0:T(8,128)(2,1)} custom-call(bf16[9,64,128]{2,1,0:T(8,128)(2,1)} %bitcast.3, bf16[8,4,128,128]{3,2,1,0:T(8,128)(2,1)} %constant.2.clone.tables_hbm, bf16[4,1,128,128]{3,2,1,0:T(8,128)(2,1)} %rot_hbm.1, bf16[40,1,128,128]{3,2,1,0:T(8,128)(2,1)} %coax_hbm.1, s32[40]{0:T(128)} %offs_ref.1, s32[40]{0:T(128)} %cls_ref.1), custom_call_target="tpu_custom_call" | custom-call | tf_op jit(solution)/shard_map/multipole_to_local/pallas_call | solution.py:354
  39.0 1.6 %copy.8 = bf16[64,9,128]{2,0,1:T(8,128)(2,1)} copy(bf16[64,9,128]{2,0,1:T(8,128)(2,1)} %bitcast.2) | data formatting | bytes 294912

commit v4 on v3

--- a/solution.py
+++ b/solution.py
@@ -10,7 +10,7 @@
 PER = 10
 COMPONENTS = 9
 CHUNKS = ((0, 4), (4, 9))
-ORDER = ("a0", "h0", "a1", "h1", "l0", "l1", "e0", "e1")
+ORDER = ("b0", "a0", "y0", "b1", "a1", "h0", "y1", "l0", "h1", "l1", "e0", "e1")
 MESH = pl.DeviceIdType.MESH
 
 
@@ -85,12 +85,12 @@
     return jnp.concatenate([split[:, h].reshape(count * 8, width) for h in range(2)], axis=0)
 
 
-def kernel(x_hbm, tables_hbm, rot_hbm, coax_hbm, offs_ref, cls_ref, out_ref, *scratch):
+def kernel(x_hbm, tables_hbm, rot_hbm, coax_hbm, offs_ref, cls_ref, out_hbm, *scratch):
     count = len(CHUNKS)
     names = ("turned", "got", "below", "above", "moved", "back")
     buffers = {name: scratch[i * count:(i + 1) * count] for i, name in enumerate(names)}
     turned, got, below, above, moved, back = (buffers[name] for name in names)
-    (x_ref, cells, tables, rot, coax, turning, turning_t, steps, chosen, load_sem, late_sem,
+    (x_ref, out_ref, cells, tables, rot, coax, turning, turning_t, steps, chosen, load_sem, out_sem, late_sem,
      fwd_send, fwd_recv, halo_send, halo_recv, bwd_send, bwd_recv) = scratch[len(names) * count:]
     cell = lax.axis_index("cell")
     coef = lax.axis_index("coef")
@@ -175,9 +175,9 @@
 
             @pl.when(jnp.logical_or(plane != 0, other != 0))
             def _():
-                send(turned[g].at[other], got[g].at[me], fwd_send.at[g], fwd_recv.at[g], device)
-
-        pltpu.make_async_copy(turned[g].at[me], got[g].at[me], fwd_recv.at[g]).start()
+                send(turned[g].at[other], got[g].at[me], fwd_send.at[g], fwd_recv.at[g, low], device)
+
+        pltpu.make_async_copy(turned[g].at[me], got[g].at[me], fwd_recv.at[g, low]).start()
 
     def greet_first():
         @pl.when(knows_first)
@@ -187,7 +187,7 @@
         @pl.when(jnp.logical_and(knows_first, plane == 0))
         def _():
             for g in range(count):
-                send(turned[g].at[0], got[g].at[me], fwd_send.at[g], fwd_recv.at[g], (0, 0))
+                send(turned[g].at[0], got[g].at[me], fwd_send.at[g], fwd_recv.at[g, low], (0, 0))
 
     def pick(k, carry):
         seen, kept = carry[0], carry[1:]
@@ -230,11 +230,15 @@
                 for m in range(2):
                     cells[s0 + m, row + j * 64:row + j * 64 + 64, :] = block[m * 64:(m + 1) * 64]
 
-    def arrive(g):
-        landed(got[g], fwd_recv.at[g])
-        send(got[g].at[pl.ds(0, 16)], above[g], halo_send.at[g, 1], halo_recv.at[g, 1], (down, coef))
-        send(got[g].at[pl.ds(16, 16)], below[g], halo_send.at[g, 0], halo_recv.at[g, 0], (up, coef))
-        lay(got[g], 128, 4, g)
+    def rise(g):
+        upper = got[g].at[pl.ds(16, 16)]
+        landed(upper, fwd_recv.at[g, 1])
+        send(upper, below[g], halo_send.at[g, 0], halo_recv.at[g, 0], (up, coef))
+
+    def sink(g):
+        lower = got[g].at[pl.ds(0, 16)]
+        landed(lower, fwd_recv.at[g, 0])
+        send(lower, above[g], halo_send.at[g, 1], halo_recv.at[g, 1], (down, coef))
 
     def translate(g, half):
         first, last = CHUNKS[g]
@@ -292,6 +296,7 @@
             piece = nn(matrix, block).T.astype(jnp.bfloat16)
             for m in range(2):
                 out_ref[s0 + m] = piece[m * 64:(m + 1) * 64]
+        pltpu.make_async_copy(out_ref.at[first:last], out_hbm.at[first:last], out_sem.at[g]).start()
 
     loads[3].wait()
     for g in range(count):
@@ -301,11 +306,12 @@
             def _():
                 pl.semaphore_wait(barrier, len(friends) - jnp.where(knows_first, 1, 0))
         spread(g)
+
     prepare_steps()
     prepare_return()
     greet_first()
     stages = {
-        "a": arrive, "h": lambda g: translate(g, 1), "l": lambda g: translate(g, 0), "e": finish,
+        "b": rise, "a": sink, "y": lambda g: lay(got[g], 128, 4, g), "h": lambda g: translate(g, 1), "l": lambda g: translate(g, 0), "e": finish,
     }
     for token in ORDER:
         stages[token[0]](int(token[1:]))
@@ -323,11 +329,13 @@
             def _():
                 landed(moved[g].at[pl.ds(0, 16)], bwd_send.at[g, half])
 
+    for g, (first, last) in enumerate(CHUNKS):
+        landed(out_ref.at[first:last], out_sem.at[g])
+
 
 def on_device(multipoles, rotation, coaxial, offsets, class_index):
     tables = jnp.asarray(block_tables(), jnp.bfloat16)
     rows = jnp.transpose(multipoles, (1, 0, 2))
-    vmem = pl.BlockSpec(memory_space=pltpu.VMEM)
     smem = pl.BlockSpec(memory_space=pltpu.SMEM)
     hbm = pl.BlockSpec(memory_space=pl.ANY)
     count = len(CHUNKS)
@@ -338,6 +346,7 @@
     dma = pltpu.SemaphoreType.DMA
     scratch += [
         pltpu.VMEM((COMPONENTS, 64, 128), bf16),
+        pltpu.VMEM((COMPONENTS, 64, 128), bf16),
         pltpu.VMEM((COMPONENTS, 512, 128), jnp.float32),
         pltpu.VMEM((4, 128, 128), bf16),
         pltpu.VMEM((NCLASS, 1, 128, 128), bf16),
@@ -346,8 +355,8 @@
         pltpu.VMEM((128, NCLASS * 128), bf16),
         pltpu.VMEM((PER, 128, 128), bf16),
         pltpu.SMEM((PER,), jnp.int32),
-        dma((4,)), pltpu.SemaphoreType.REGULAR,
-        dma((count,)), dma((count,)),
+        dma((4,)), dma((count,)), pltpu.SemaphoreType.REGULAR,
+        dma((count,)), dma((count, 2)),
         dma((count, 2)), dma((count, 2)),
         dma((count, 2)), dma((count,)),
     ]
@@ -355,7 +364,7 @@
         kernel,
         out_shape=jax.ShapeDtypeStruct((COMPONENTS, 64, 128), bf16),
         in_specs=[hbm, hbm, hbm, hbm, smem, smem],
-        out_specs=vmem,
+        out_specs=hbm,
         scratch_shapes=scratch,
         compiler_params=pltpu.CompilerParams(collective_id=0, has_side_effects=True),
         name="multipole_to_local",

time: 41.1 us -> 39.2 us (0.954)
  Pallas kernels: 38.9 us -> 37.4 us
    pallas_call x1, Pallas kernels: 38.9 us -> 37.4 us  [on_device(): pl.pallas_call(kernel, out_shape=jax.ShapeDtypeStruct((COMPONENTS, 64, 12...]
where the time goes in v4:
time: 39.2 us; the launch traced here: 39 us
  Pallas kernels  37.4 us (95%)
  local copies, waits for them, and re-layouts  1.58 us (4%)
    pallas_call x1, Pallas kernels, on_device(): pl.pallas_call(kernel, out_shape=jax.ShapeDtypeStruct((COMPONENTS, 64, 12...  37.4 us
    unnamed x1, local copies, waits for them, and re-layouts  1.58 us

profile of v4, /device:TPU:1, one launch (start us, length us, event | category | flops | bytes accessed | tf_op | source)
XLA Modules:
  0.0 39.0 jit_solution(16011521613465744133)
XLA Ops:
  0.0 37.4 %multipole_to_local.1 = bf16[9,64,128]{2,1,0:T(8,128)(2,1)} custom-call(bf16[9,64,128]{2,1,0:T(8,128)(2,1)} %bitcast.3, bf16[8,4,128,128]{3,2,1,0:T(8,128)(2,1)} %constant.2.clone.tables_hbm, bf16[4,1,128,128]{3,2,1,0:T(8,128)(2,1)} %rot_hbm.1, bf16[40,1,128,128]{3,2,1,0:T(8,128)(2,1)} %coax_hbm.1, s32[40]{0:T(128)} %offs_ref.1, s32[40]{0:T(128)} %cls_ref.1), custom_call_target="tpu_custom_call" | custom-call | tf_op jit(solution)/shard_map/multipole_to_local/pallas_call | solution.py:363
  37.4 1.6 %copy.8 = bf16[64,9,128]{2,0,1:T(8,128)(2,1)} copy(bf16[64,9,128]{2,0,1:T(8,128)(2,1)} %bitcast.2) | data formatting | bytes 294912

commit v5 on v4

--- a/solution.py
+++ b/solution.py
@@ -9,8 +9,11 @@
 NCLASS = 4
 PER = 10
 COMPONENTS = 9
-CHUNKS = ((0, 4), (4, 9))
-ORDER = ("b0", "a0", "y0", "b1", "a1", "h0", "y1", "l0", "h1", "l1", "e0", "e1")
+CHUNKS = ((0, 2), (2, 6), (6, 9))
+ORDER = (
+    "b0", "a0", "y0", "b1", "a1", "y1", "h0", "b2", "a2", "l0",
+    "h1", "y2", "l1", "h2", "l2", "e0", "e1", "e2",
+)
 MESH = pl.DeviceIdType.MESH
 
 
@@ -85,12 +88,12 @@
     return jnp.concatenate([split[:, h].reshape(count * 8, width) for h in range(2)], axis=0)
 
 
-def kernel(x_hbm, tables_hbm, rot_hbm, coax_hbm, offs_ref, cls_ref, out_hbm, *scratch):
+def kernel(x_hbm, tables_hbm, rot_hbm, coax_hbm, offs_hbm, cls_hbm, out_hbm, *scratch):
     count = len(CHUNKS)
     names = ("turned", "got", "below", "above", "moved", "back")
     buffers = {name: scratch[i * count:(i + 1) * count] for i, name in enumerate(names)}
     turned, got, below, above, moved, back = (buffers[name] for name in names)
-    (x_ref, out_ref, cells, tables, rot, coax, turning, turning_t, steps, chosen, load_sem, out_sem, late_sem,
+    (offs_ref, cls_ref, x_ref, out_ref, cells, tables, rot, coax, turning, turning_t, steps, chosen, load_sem, out_sem, late_sem,
      fwd_send, fwd_recv, halo_send, halo_recv, bwd_send, bwd_recv) = scratch[len(names) * count:]
     cell = lax.axis_index("cell")
     coef = lax.axis_index("coef")
@@ -133,8 +136,10 @@
         pltpu.make_async_copy(rot_hbm, rot, load_sem.at[1]),
         pltpu.make_async_copy(coax_hbm, coax, load_sem.at[2]),
         pltpu.make_async_copy(x_hbm, x_ref, load_sem.at[3]),
+        pltpu.make_async_copy(offs_hbm, offs_ref, load_sem.at[4]),
+        pltpu.make_async_copy(cls_hbm, cls_ref, load_sem.at[5]),
     ]
-    for load in (loads[0], loads[1], loads[3], loads[2]):
+    for load in (loads[0], loads[1], loads[3], loads[2], loads[4], loads[5]):
         load.start()
 
     @pl.when(is_first)
@@ -197,6 +202,8 @@
         return (seen + jnp.where(hit, 1, 0),) + kept
 
     def prepare_steps():
+        loads[4].wait()
+        loads[5].wait()
         picked = lax.fori_loop(0, NCLASS * PER, pick, (jnp.int32(0),) * (PER + 1))[1:]
         for p in range(PER):
             chosen[p] = picked[p]
@@ -336,7 +343,6 @@
 def on_device(multipoles, rotation, coaxial, offsets, class_index):
     tables = jnp.asarray(block_tables(), jnp.bfloat16)
     rows = jnp.transpose(multipoles, (1, 0, 2))
-    smem = pl.BlockSpec(memory_space=pltpu.SMEM)
     hbm = pl.BlockSpec(memory_space=pl.ANY)
     count = len(CHUNKS)
     bf16 = jnp.bfloat16
@@ -345,6 +351,8 @@
         scratch += [pltpu.VMEM((outer, tiles(g), 8, 128), bf16) for g in range(count)]
     dma = pltpu.SemaphoreType.DMA
     scratch += [
+        pltpu.SMEM((NCLASS * PER,), jnp.int32),
+        pltpu.SMEM((NCLASS * PER,), jnp.int32),
         pltpu.VMEM((COMPONENTS, 64, 128), bf16),
         pltpu.VMEM((COMPONENTS, 64, 128), bf16),
         pltpu.VMEM((COMPONENTS, 512, 128), jnp.float32),
@@ -355,7 +363,7 @@
         pltpu.VMEM((128, NCLASS * 128), bf16),
         pltpu.VMEM((PER, 128, 128), bf16),
         pltpu.SMEM((PER,), jnp.int32),
-        dma((4,)), dma((count,)), pltpu.SemaphoreType.REGULAR,
+        dma((6,)), dma((count,)), pltpu.SemaphoreType.REGULAR,
         dma((count,)), dma((count, 2)),
         dma((count, 2)), dma((count, 2)),
         dma((count, 2)), dma((count,)),
@@ -363,7 +371,7 @@
     field = pl.pallas_call(
         kernel,
         out_shape=jax.ShapeDtypeStruct((COMPONENTS, 64, 128), bf16),
-        in_specs=[hbm, hbm, hbm, hbm, smem, smem],
+        in_specs=[hbm] * 6,
         out_specs=hbm,
         scratch_shapes=scratch,
         compiler_params=pltpu.CompilerParams(collective_id=0, has_side_effects=True),

time: 39.2 us -> 38.5 us (0.982)
  Pallas kernels: 37.4 us -> 36.8 us
    pallas_call x1, Pallas kernels: 37.4 us -> 36.8 us  [on_device(): pl.pallas_call(kernel, out_shape=jax.ShapeDtypeStruct((COMPONENTS, 64, 12...]
where the time goes in v5:
time: 38.5 us; the launch traced here: 38.4 us
  Pallas kernels  36.8 us (96%)
  local copies, waits for them, and re-layouts  1.58 us (4%)
    pallas_call x1, Pallas kernels, on_device(): pl.pallas_call(kernel, out_shape=jax.ShapeDtypeStruct((COMPONENTS, 64, 12...  36.8 us
    unnamed x1, local copies, waits for them, and re-layouts  1.58 us

profile of v5, /device:TPU:1, one launch (start us, length us, event | category | flops | bytes accessed | tf_op | source)
XLA Modules:
  0.0 38.4 jit_solution(67507845283436390)
XLA Ops:
  0.0 36.8 %multipole_to_local.1 = bf16[9,64,128]{2,1,0:T(8,128)(2,1)} custom-call(bf16[9,64,128]{2,1,0:T(8,128)(2,1)} %bitcast.3, bf16[8,4,128,128]{3,2,1,0:T(8,128)(2,1)} %constant.2.clone.tables_hbm, bf16[4,1,128,128]{3,2,1,0:T(8,128)(2,1)} %rot_hbm.1, bf16[40,1,128,128]{3,2,1,0:T(8,128)(2,1)} %coax_hbm.1, s32[40]{0:T(128)} %offs_hbm.1, s32[40]{0:T(128)} %cls_hbm.1), custom_call_target="tpu_custom_call" | custom-call | tf_op jit(solution)/shard_map/multipole_to_local/pallas_call | solution.py:371
  36.8 1.6 %copy.8 = bf16[64,9,128]{2,0,1:T(8,128)(2,1)} copy(bf16[64,9,128]{2,0,1:T(8,128)(2,1)} %bitcast.2) | data formatting | bytes 294912

commit v6 on v5

--- a/solution.py
+++ b/solution.py
@@ -88,12 +88,12 @@
     return jnp.concatenate([split[:, h].reshape(count * 8, width) for h in range(2)], axis=0)
 
 
-def kernel(x_hbm, tables_hbm, rot_hbm, coax_hbm, offs_hbm, cls_hbm, out_hbm, *scratch):
+def kernel(x_hbm, tables_hbm, rot_hbm, coax_hbm, offs_hbm, cls_hbm, out_ref, *scratch):
     count = len(CHUNKS)
     names = ("turned", "got", "below", "above", "moved", "back")
     buffers = {name: scratch[i * count:(i + 1) * count] for i, name in enumerate(names)}
     turned, got, below, above, moved, back = (buffers[name] for name in names)
-    (offs_ref, cls_ref, x_ref, out_ref, cells, tables, rot, coax, turning, turning_t, steps, chosen, load_sem, out_sem, late_sem,
+    (offs_ref, cls_ref, x_ref, cells, tables, rot, coax, turning, turning_t, steps, chosen, load_sem, late_sem,
      fwd_send, fwd_recv, halo_send, halo_recv, bwd_send, bwd_recv) = scratch[len(names) * count:]
     cell = lax.axis_index("cell")
     coef = lax.axis_index("coef")
@@ -303,7 +303,6 @@
             piece = nn(matrix, block).T.astype(jnp.bfloat16)
             for m in range(2):
                 out_ref[s0 + m] = piece[m * 64:(m + 1) * 64]
-        pltpu.make_async_copy(out_ref.at[first:last], out_hbm.at[first:last], out_sem.at[g]).start()
 
     loads[3].wait()
     for g in range(count):
@@ -335,10 +334,6 @@
             @pl.when(low != half)
             def _():
                 landed(moved[g].at[pl.ds(0, 16)], bwd_send.at[g, half])
-
-    for g, (first, last) in enumerate(CHUNKS):
-        landed(out_ref.at[first:last], out_sem.at[g])
-
 
 def on_device(multipoles, rotation, coaxial, offsets, class_index):
     tables = jnp.asarray(block_tables(), jnp.bfloat16)
@@ -354,7 +349,6 @@
         pltpu.SMEM((NCLASS * PER,), jnp.int32),
         pltpu.SMEM((NCLASS * PER,), jnp.int32),
         pltpu.VMEM((COMPONENTS, 64, 128), bf16),
-        pltpu.VMEM((COMPONENTS, 64, 128), bf16),
         pltpu.VMEM((COMPONENTS, 512, 128), jnp.float32),
         pltpu.VMEM((4, 128, 128), bf16),
         pltpu.VMEM((NCLASS, 1, 128, 128), bf16),
@@ -363,16 +357,16 @@
         pltpu.VMEM((128, NCLASS * 128), bf16),
         pltpu.VMEM((PER, 128, 128), bf16),
         pltpu.SMEM((PER,), jnp.int32),
-        dma((6,)), dma((count,)), pltpu.SemaphoreType.REGULAR,
+        dma((6,)), pltpu.SemaphoreType.REGULAR,
         dma((count,)), dma((count, 2)),
         dma((count, 2)), dma((count, 2)),
         dma((count, 2)), dma((count,)),
     ]
     field = pl.pallas_call(
         kernel,
-        out_shape=jax.ShapeDtypeStruct((COMPONENTS, 64, 128), bf16),
+        out_shape=pltpu.VMEM((COMPONENTS, 64, 128), bf16),
         in_specs=[hbm] * 6,
-        out_specs=hbm,
+        out_specs=pl.BlockSpec(memory_space=pltpu.VMEM),
         scratch_shapes=scratch,
         compiler_params=pltpu.CompilerParams(collective_id=0, has_side_effects=True),
         name="multipole_to_local",

time: 38.5 us -> 37 us (0.961)
  local copies, waits for them, and re-layouts: 1.58 us -> 0.66 us
  Pallas kernels: 36.8 us -> 36.2 us
    unnamed x1, local copies, waits for them, and re-layouts: 1.58 us -> 0.66 us
    pallas_call x1, Pallas kernels: 36.8 us -> 36.2 us  [on_device(): pl.pallas_call(kernel, out_shape=pltpu.VMEM((COMPONENTS, 64, 128), bf16),...]
where the time goes in v6:
time: 37 us; the launch traced here: 36.9 us
  Pallas kernels  36.2 us (98%)
  local copies, waits for them, and re-layouts  0.66 us (2%)
    pallas_call x1, Pallas kernels, on_device(): pl.pallas_call(kernel, out_shape=pltpu.VMEM((COMPONENTS, 64, 128), bf16),...  36.2 us

profile of v6, /device:TPU:1, one launch (start us, length us, event | category | flops | bytes accessed | tf_op | source)
XLA Modules:
  0.0 36.9 jit_solution(7101784084699868126)
XLA Ops:
  0.0 36.2 %multipole_to_local.1 = bf16[9,64,128]{2,1,0:T(8,128)(2,1)S(1)} custom-call(bf16[9,64,128]{2,1,0:T(8,128)(2,1)} %bitcast.3, bf16[8,4,128,128]{3,2,1,0:T(8,128)(2,1)} %constant.2.clone.tables_hbm, bf16[4,1,128,128]{3,2,1,0:T(8,128)(2,1)} %rot_hbm.1, bf16[40,1,128,128]{3,2,1,0:T(8,128)(2,1)} %coax_hbm.1, s32[40]{0:T(128)} %offs_hbm.1, s32[40]{0:T(128)} %cls_hbm.1), custom_call_target="tpu_custom_call" | custom-call | tf_op jit(solution)/shard_map/multipole_to_local/pallas_call | solution.py:365
  36.2 0.7 %copy.8 = bf16[64,9,128]{2,0,1:T(8,128)(2,1)} copy(bf16[64,9,128]{2,0,1:T(8,128)(2,1)S(1)} %bitcast.2) | data formatting | bytes 294912

commit v7 on v6

--- a/solution.py
+++ b/solution.py
@@ -11,8 +11,7 @@
 COMPONENTS = 9
 CHUNKS = ((0, 2), (2, 6), (6, 9))
 ORDER = (
-    "b0", "a0", "y0", "b1", "a1", "y1", "h0", "b2", "a2", "l0",
-    "h1", "y2", "l1", "h2", "l2", "e0", "e1", "e2",
+    "b0", "a0", "y0", "b1", "a1", "b2", "a2", "y1", "h0", "h1", "l0", "y2", "h2", "l1", "l2", "e0", "e1", "e2",
 )
 MESH = pl.DeviceIdType.MESH
 

time: 37 us -> 36.7 us (level)
  no operation moved by 1% of the time
where the time goes in v7:
time: 36.7 us; the launch traced here: 36.6 us
  Pallas kernels  35.9 us (98%)
  local copies, waits for them, and re-layouts  0.66 us (2%)
    pallas_call x1, Pallas kernels, on_device(): pl.pallas_call(kernel, out_shape=pltpu.VMEM((COMPONENTS, 64, 128), bf16),...  35.9 us

profile of v7, /device:TPU:1, one launch (start us, length us, event | category | flops | bytes accessed | tf_op | source)
XLA Modules:
  0.0 36.6 jit_solution(17952211988261598430)
XLA Ops:
  0.0 35.9 %multipole_to_local.1 = bf16[9,64,128]{2,1,0:T(8,128)(2,1)S(1)} custom-call(bf16[9,64,128]{2,1,0:T(8,128)(2,1)} %bitcast.3, bf16[8,4,128,128]{3,2,1,0:T(8,128)(2,1)} %constant.2.clone.tables_hbm, bf16[4,1,128,128]{3,2,1,0:T(8,128)(2,1)} %rot_hbm.1, bf16[40,1,128,128]{3,2,1,0:T(8,128)(2,1)} %coax_hbm.1, s32[40]{0:T(128)} %offs_hbm.1, s32[40]{0:T(128)} %cls_hbm.1), custom_call_target="tpu_custom_call" | custom-call | tf_op jit(solution)/shard_map/multipole_to_local/pallas_call | solution.py:364
  35.9 0.7 %copy.8 = bf16[64,9,128]{2,0,1:T(8,128)(2,1)} copy(bf16[64,9,128]{2,0,1:T(8,128)(2,1)S(1)} %bitcast.2) | data formatting | bytes 294912

commit v8 on v7

--- a/solution.py
+++ b/solution.py
@@ -9,7 +9,7 @@
 NCLASS = 4
 PER = 10
 COMPONENTS = 9
-CHUNKS = ((0, 2), (2, 6), (6, 9))
+CHUNKS = ((0, 3), (3, 7), (7, 9))
 ORDER = (
     "b0", "a0", "y0", "b1", "a1", "b2", "a2", "y1", "h0", "h1", "l0", "y2", "h2", "l1", "l2", "e0", "e1", "e2",
 )

time: 36.7 us -> 36.3 us (0.989)
  no operation moved by 1% of the time
where the time goes in v8:
time: 36.3 us; the launch traced here: 36.2 us
  Pallas kernels  35.6 us (98%)
  local copies, waits for them, and re-layouts  0.66 us (2%)
    pallas_call x1, Pallas kernels, on_device(): pl.pallas_call(kernel, out_shape=pltpu.VMEM((COMPONENTS, 64, 128), bf16),...  35.6 us

profile of v8, /device:TPU:1, one launch (start us, length us, event | category | flops | bytes accessed | tf_op | source)
XLA Modules:
  0.0 36.2 jit_solution(17131826743083551476)
XLA Ops:
  0.0 35.6 %multipole_to_local.1 = bf16[9,64,128]{2,1,0:T(8,128)(2,1)S(1)} custom-call(bf16[9,64,128]{2,1,0:T(8,128)(2,1)} %bitcast.3, bf16[8,4,128,128]{3,2,1,0:T(8,128)(2,1)} %constant.2.clone.tables_hbm, bf16[4,1,128,128]{3,2,1,0:T(8,128)(2,1)} %rot_hbm.1, bf16[40,1,128,128]{3,2,1,0:T(8,128)(2,1)} %coax_hbm.1, s32[40]{0:T(128)} %offs_hbm.1, s32[40]{0:T(128)} %cls_hbm.1), custom_call_target="tpu_custom_call" | custom-call | tf_op jit(solution)/shard_map/multipole_to_local/pallas_call | solution.py:364
  35.6 0.7 %copy.8 = bf16[64,9,128]{2,0,1:T(8,128)(2,1)} copy(bf16[64,9,128]{2,0,1:T(8,128)(2,1)S(1)} %bitcast.2) | data formatting | bytes 294912

commit v9 on v8

--- a/solution.py
+++ b/solution.py
@@ -174,12 +174,23 @@
                     turned[g][:, 2 * at + h] = result[:, h].astype(jnp.bfloat16)
 
     def spread(g):
-        for step in FAR_FIRST:
-            other, device = partner(*step)
-
-            @pl.when(jnp.logical_or(plane != 0, other != 0))
-            def _():
-                send(turned[g].at[other], got[g].at[me], fwd_send.at[g], fwd_recv.at[g, low], device)
+        def each(guarded):
+            for step in FAR_FIRST:
+                other, device = partner(*step)
+                if guarded:
+                    @pl.when(other != 0)
+                    def _():
+                        send(turned[g].at[other], got[g].at[me], fwd_send.at[g], fwd_recv.at[g, low], device)
+                else:
+                    send(turned[g].at[other], got[g].at[me], fwd_send.at[g], fwd_recv.at[g, low], device)
+
+        @pl.when(plane != 0)
+        def _():
+            each(False)
+
+        @pl.when(plane == 0)
+        def _():
+            each(True)
 
         pltpu.make_async_copy(turned[g].at[me], got[g].at[me], fwd_recv.at[g, low]).start()
 

time: 36.3 us -> 36.3 us (level)
  no operation moved by 1% of the time
where the time goes in v9:
time: 36.3 us; the launch traced here: 36.2 us
  Pallas kernels  35.5 us (98%)
  local copies, waits for them, and re-layouts  0.66 us (2%)
    pallas_call x1, Pallas kernels, on_device(): pl.pallas_call(kernel, out_shape=pltpu.VMEM((COMPONENTS, 64, 128), bf16),...  35.5 us

profile of v9, /device:TPU:1, one launch (start us, length us, event | category | flops | bytes accessed | tf_op | source)
XLA Modules:
  0.0 36.2 jit_solution(9159308558883375880)
XLA Ops:
  0.0 35.5 %multipole_to_local.1 = bf16[9,64,128]{2,1,0:T(8,128)(2,1)S(1)} custom-call(bf16[9,64,128]{2,1,0:T(8,128)(2,1)} %bitcast.3, bf16[8,4,128,128]{3,2,1,0:T(8,128)(2,1)} %constant.2.clone.tables_hbm, bf16[4,1,128,128]{3,2,1,0:T(8,128)(2,1)} %rot_hbm.1, bf16[40,1,128,128]{3,2,1,0:T(8,128)(2,1)} %coax_hbm.1, s32[40]{0:T(128)} %offs_hbm.1, s32[40]{0:T(128)} %cls_hbm.1), custom_call_target="tpu_custom_call" | custom-call | tf_op jit(solution)/shard_map/multipole_to_local/pallas_call | solution.py:375
  35.6 0.7 %copy.8 = bf16[64,9,128]{2,0,1:T(8,128)(2,1)} copy(bf16[64,9,128]{2,0,1:T(8,128)(2,1)S(1)} %bitcast.2) | data formatting | bytes 294912
